TPU v7x, 128 devices: a whole 4x4x4 slice. The times are simulated.
128 devices in a mesh: chan: 32 (over x, z_hi, y), grp: 4 (over z_lo, core).
Axes of the slice: x: 4, y: 4, z: 4 (z_hi: 2, z_lo: 2; z = z_hi * 2 + z_lo), core: 2. Of those that a mesh axis runs over, the one named last changes fastest.
Arguments:
- voltages: bfloat16 [512, 4096, 128], P(('chan', 'grp')), may hold values from -6 to 6
- delays: int32 [64, 512], replicated, may hold values from 0 to 4095
- shifts: int32 [256, 512], replicated, may hold values from 0 to 511
Outputs:
- dm_power: float32 [256, 512, 256], P('grp', 'chan')
All inputs are finite; a program needn't handle non-finite values.
Results may differ from a plain program's by a relative error of at most 0.011.
Values may be sent and summed in bfloat16 or wider, within the bound.
No kernel may reach another device: no remote copies, remote signals or barrier semaphores. Data moves between devices by JAX's collectives and lax.ppermute only.
A program may use at most 128 MiB of HBM per device.

v0:
```python
import math

import jax
import jax.numpy as jnp
from jax import lax
from jax.sharding import PartitionSpec as P

DISHES = 64
INTEG = 8
PHASES = 4096
KBLK = 16


def beam_matrix(delays, channel, channel_count):
    frequency = channel + channel_count
    residue = jnp.mod(delays * frequency, PHASES)
    phases = residue.astype(jnp.float32) * jnp.float32(2.0 * math.pi / PHASES)
    weight_scale = jnp.float32(1.0 / math.sqrt(DISHES))
    real_part = jnp.cos(phases) * weight_scale
    imag_part = -jnp.sin(phases) * weight_scale
    upper = jnp.concatenate([real_part, imag_part], axis=1)
    lower = jnp.concatenate([-imag_part, real_part], axis=1)
    return jnp.concatenate([upper, lower], axis=0).astype(jnp.bfloat16)


def detect(samples, matrix):
    beams = jnp.dot(samples, matrix, preferred_element_type=jnp.float32)
    half_width = matrix.shape[1] // 2
    intensity = beams[:, :half_width] ** 2 + beams[:, half_width:] ** 2
    steps_count = samples.shape[0] // INTEG
    averaged = jnp.sum(intensity.reshape(steps_count, INTEG, half_width), axis=1) * jnp.float32(
        1.0 / INTEG
    )
    return averaged.T.astype(jnp.bfloat16)


def dft_table(length):
    bins_count = length // 2
    sample_index = jnp.arange(length, dtype=jnp.int32)[:, None]
    freq_index = jnp.arange(1, bins_count + 1, dtype=jnp.int32)[None, :]
    residue = jnp.mod(sample_index * freq_index, length)
    phases = residue.astype(jnp.float32) * jnp.float32(2.0 * math.pi / length)
    norm_scale = jnp.float32(1.0 / math.sqrt(length))
    return jnp.concatenate(
        [jnp.cos(phases) * norm_scale, -jnp.sin(phases) * norm_scale], axis=1
    ).astype(jnp.bfloat16)


def spectra(series, table):
    flat = series.reshape(-1, series.shape[-1])
    result = jnp.dot(flat, table, preferred_element_type=jnp.float32).astype(jnp.bfloat16)
    return result.reshape(series.shape[:-1] + (table.shape[1],))


def dedisperse(spectrum, selected, phase_scale):
    channel_count, beam_count, doubled = spectrum.shape
    bins_count = doubled // 2
    trial_count = selected.shape[0]
    parted = spectrum.reshape(channel_count, beam_count, 2, bins_count).transpose(2, 3, 1, 0)
    real_spec = parted[0]
    imag_spec = parted[1]
    across = selected.T

    def one_block(block_index):
        start = block_index * KBLK
        real_piece = lax.dynamic_slice_in_dim(real_spec, start, KBLK, 0)
        imag_piece = lax.dynamic_slice_in_dim(imag_spec, start, KBLK, 0)
        freq_index = (start + jnp.arange(KBLK, dtype=jnp.int32) + 1)[:, None, None]
        residue = jnp.mod(freq_index * across[None, :, :], doubled)
        phases = residue.astype(jnp.float32) * jnp.float32(2.0 * math.pi / doubled)
        cosine = (jnp.cos(phases) * phase_scale).astype(jnp.bfloat16)
        sine = (jnp.sin(phases) * phase_scale).astype(jnp.bfloat16)
        cos_real = jnp.einsum(
            "kbc,kcm->kbm", real_piece, cosine, preferred_element_type=jnp.float32
        )
        sin_imag = jnp.einsum("kbc,kcm->kbm", imag_piece, sine, preferred_element_type=jnp.float32)
        sin_real = jnp.einsum("kbc,kcm->kbm", real_piece, sine, preferred_element_type=jnp.float32)
        cos_imag = jnp.einsum(
            "kbc,kcm->kbm", imag_piece, cosine, preferred_element_type=jnp.float32
        )
        return jnp.stack([cos_real - sin_imag, sin_real + cos_imag], axis=1)

    blocks = lax.map(one_block, jnp.arange(bins_count // KBLK, dtype=jnp.int32))
    return blocks.reshape(bins_count, 2, beam_count, trial_count)


def body(voltages, delays, shifts):
    chan_count = lax.axis_size("chan")
    group_count = lax.axis_size("grp")
    chan_local = voltages.shape[0]
    channel_total = chan_local * chan_count * group_count
    first_channel = (lax.axis_index("chan") * group_count + lax.axis_index("grp")) * chan_local

    def detect_channel(item):
        samples, offset = item
        return detect(samples, beam_matrix(delays, first_channel + offset, channel_total))

    detected = lax.map(detect_channel, (voltages, jnp.arange(chan_local, dtype=jnp.int32)))
    table = dft_table(detected.shape[2])
    phase_scale = jnp.float32(1.0 / math.sqrt(channel_total))
    trial_count = shifts.shape[0]
    grouped = shifts.reshape(trial_count, chan_count, group_count, chan_local)
    selected = lax.dynamic_index_in_dim(grouped, lax.axis_index("grp"), axis=2, keepdims=False)
    selected = selected.reshape(trial_count, chan_count * chan_local)
    beam_total = detected.shape[1]
    blocked = detected.reshape(chan_local, chan_count, beam_total // chan_count, detected.shape[2])
    partial_spec = dedisperse(
        spectra(
            lax.all_to_all(blocked, "chan", split_axis=1, concat_axis=0, tiled=True)[:, 0], table
        ),
        selected,
        phase_scale,
    )
    summed = lax.psum_scatter(partial_spec, "grp", scatter_dimension=3, tiled=True)
    result = summed[:, 0] ** 2 + summed[:, 1] ** 2
    return result.transpose(2, 1, 0)


def solution(mesh):
    placed = (P(("chan", "grp"), None, None), P(), P())
    return jax.shard_map(
        body, mesh=mesh, in_specs=placed, out_specs=P("grp", "chan", None), check_vma=False
    )
```

profile of v0, /device:TPU:1, one launch (start us, length us, event | category | flops | bytes accessed | tf_op | source)
XLA Modules:
  0.0 781.8 jit_solution(4878138713700647623)
XLA Ops:
  6.5 39.4 %while.24 = (s32[]{:T(128)}, bf16[4,512,512]{2,1,0:T(8,128)(2,1)S(1)}, bf16[4,4096,128]{2,1,0:T(8,128)(2,1)}, s32[4]{0:T(128)S(1)}, s32[]{:T(128)}, /*index=5*/s32[64,512]{1,0:T(8,128)}, s32[]{:T(128)}, s32[]{:T(128)}) while((s32[]{:T(128)}, bf16[4,512,512]{2,1,0:T(8,128)(2,1)S(1)}, bf16[4,4096,128]{2,1,0:T(8,128)(2,1)}, s32[4]{0:T(128)S(1)}, ...), condition=%wide.region_2.3_spmd, body=%wide.region_0.2_spmd.sunk | while | flops 1084129280 | bytes 39846528 | solution.py:98
  47.6 11.3 %all-to-all-start = ((bf16[4,32,16,512]{3,2,0,1:T(8,128)(2,1)}), bf16[4,32,16,512]{3,2,0,1:T(8,128)(2,1)S(1)}, u32[]{:S(2)}, u32[]{:S(2)}) async-start(bf16[4,32,16,512]{3,2,0,1:T(8,128)(2,1)} %copy.17), calls=%async_computation | async-start | bytes 4194304 | tf_op jit(solution)/shard_map/all_to_all | solution.py:109
  61.7 25.5 %all-to-all-done = bf16[4,32,16,512]{3,2,0,1:T(8,128)(2,1)S(1)} async-done(((bf16[4,32,16,512]{3,2,0,1:T(8,128)(2,1)}), bf16[4,32,16,512]{3,2,0,1:T(8,128)(2,1)S(1)}, u32[]{:S(2)}, u32[]{:S(2)}) %all-to-all-start) | async-done | bytes 2097184 | tf_op jit(solution)/shard_map/all_to_all | solution.py:109
  99.1 583.7 %while.25 = (s32[]{:T(128)}, f32[16,16,2,16,256]{4,3,2,1,0:T(8,128)}, s32[16]{0:T(128)S(1)}, bf16[256,16,128]{2,1,0:T(8,128)(2,1)}, s32[128,256]{1,0:T(8,128)S(1...) while((s32[]{:T(128)}, f32[16,16,2,16,256]{4,3,2,1,0:T(8,128)}, ...), condition=%wide.region_4.5_spmd, body=%wide.region_3.4_spmd.sunk | while | flops 100925472 | bytes 3409779 | solution.py:83
  138.8 8.7 %fusion.88 = f32[16,16,256]{2,1,0:T(8,128)S(1)} fusion(s32[128,256]{1,0:T(8,128)S(1)} %get-tuple-element.322, s32[16]{0:T(128)S(1)} %add_add_fusion.2, bf16[256,16,128]{2,1,0:T(8,128)(2,1)} %get-tuple-element.321, s32[]{:T(128)S(6)} %select_n.88), kind=kOutput, calls=%fused_computation.45.clone.1 | convolution fusion | flops 25165824 | bytes 458820 | tf_op jit(solution)/shard_map/while/body/eval_jaxpr/kbc,kcm->kbm/dot_general | solution.py:77
  173.9 8.7 %fusion.88 = f32[16,16,256]{2,1,0:T(8,128)S(1)} fusion(s32[128,256]{1,0:T(8,128)S(1)} %get-tuple-element.322, s32[16]{0:T(128)S(1)} %add_add_fusion.2, bf16[256,16,128]{2,1,0:T(8,128)(2,1)} %get-tuple-element.321, s32[]{:T(128)S(6)} %select_n.88), kind=kOutput, calls=%fused_computation.45.clone.1 | convolution fusion | flops 25165824 | bytes 458820 | tf_op jit(solution)/shard_map/while/body/eval_jaxpr/kbc,kcm->kbm/dot_general | solution.py:77
  209.0 8.7 %fusion.88 = f32[16,16,256]{2,1,0:T(8,128)S(1)} fusion(s32[128,256]{1,0:T(8,128)S(1)} %get-tuple-element.322, s32[16]{0:T(128)S(1)} %add_add_fusion.2, bf16[256,16,128]{2,1,0:T(8,128)(2,1)} %get-tuple-element.321, s32[]{:T(128)S(6)} %select_n.88), kind=kOutput, calls=%fused_computation.45.clone.1 | convolution fusion | flops 25165824 | bytes 458820 | tf_op jit(solution)/shard_map/while/body/eval_jaxpr/kbc,kcm->kbm/dot_general | solution.py:77
  244.1 8.7 %fusion.88 = f32[16,16,256]{2,1,0:T(8,128)S(1)} fusion(s32[128,256]{1,0:T(8,128)S(1)} %get-tuple-element.322, s32[16]{0:T(128)S(1)} %add_add_fusion.2, bf16[256,16,128]{2,1,0:T(8,128)(2,1)} %get-tuple-element.321, s32[]{:T(128)S(6)} %select_n.88), kind=kOutput, calls=%fused_computation.45.clone.1 | convolution fusion | flops 25165824 | bytes 458820 | tf_op jit(solution)/shard_map/while/body/eval_jaxpr/kbc,kcm->kbm/dot_general | solution.py:77
  262.7 8.6 %fusion.90 = f32[16,16,256]{2,1,0:T(8,128)S(1)} fusion(s32[128,256]{1,0:T(8,128)S(1)} %get-tuple-element.322, s32[16]{0:T(128)S(1)} %add_add_fusion.2, bf16[256,16,128]{2,1,0:T(8,128)(2,1)} %get-tuple-element.321, s32[]{:T(128)S(6)} %select_n.88), kind=kOutput, calls=%fused_computation.44.clone.1 | convolution fusion | flops 25165824 | bytes 458820 | tf_op jit(solution)/shard_map/while/body/eval_jaxpr/kbc,kcm->kbm/dot_general | solution.py:73
  279.2 8.7 %fusion.88 = f32[16,16,256]{2,1,0:T(8,128)S(1)} fusion(s32[128,256]{1,0:T(8,128)S(1)} %get-tuple-element.322, s32[16]{0:T(128)S(1)} %add_add_fusion.2, bf16[256,16,128]{2,1,0:T(8,128)(2,1)} %get-tuple-element.321, s32[]{:T(128)S(6)} %select_n.88), kind=kOutput, calls=%fused_computation.45.clone.1 | convolution fusion | flops 25165824 | bytes 458820 | tf_op jit(solution)/shard_map/while/body/eval_jaxpr/kbc,kcm->kbm/dot_general | solution.py:77
  297.8 8.6 %fusion.90 = f32[16,16,256]{2,1,0:T(8,128)S(1)} fusion(s32[128,256]{1,0:T(8,128)S(1)} %get-tuple-element.322, s32[16]{0:T(128)S(1)} %add_add_fusion.2, bf16[256,16,128]{2,1,0:T(8,128)(2,1)} %get-tuple-element.321, s32[]{:T(128)S(6)} %select_n.88), kind=kOutput, calls=%fused_computation.44.clone.1 | convolution fusion | flops 25165824 | bytes 458820 | tf_op jit(solution)/shard_map/while/body/eval_jaxpr/kbc,kcm->kbm/dot_general | solution.py:73
  314.3 8.7 %fusion.88 = f32[16,16,256]{2,1,0:T(8,128)S(1)} fusion(s32[128,256]{1,0:T(8,128)S(1)} %get-tuple-element.322, s32[16]{0:T(128)S(1)} %add_add_fusion.2, bf16[256,16,128]{2,1,0:T(8,128)(2,1)} %get-tuple-element.321, s32[]{:T(128)S(6)} %select_n.88), kind=kOutput, calls=%fused_computation.45.clone.1 | convolution fusion | flops 25165824 | bytes 458820 | tf_op jit(solution)/shard_map/while/body/eval_jaxpr/kbc,kcm->kbm/dot_general | solution.py:77
  349.4 8.7 %fusion.88 = f32[16,16,256]{2,1,0:T(8,128)S(1)} fusion(s32[128,256]{1,0:T(8,128)S(1)} %get-tuple-element.322, s32[16]{0:T(128)S(1)} %add_add_fusion.2, bf16[256,16,128]{2,1,0:T(8,128)(2,1)} %get-tuple-element.321, s32[]{:T(128)S(6)} %select_n.88), kind=kOutput, calls=%fused_computation.45.clone.1 | convolution fusion | flops 25165824 | bytes 458820 | tf_op jit(solution)/shard_map/while/body/eval_jaxpr/kbc,kcm->kbm/dot_general | solution.py:77
  384.5 8.7 %fusion.88 = f32[16,16,256]{2,1,0:T(8,128)S(1)} fusion(s32[128,256]{1,0:T(8,128)S(1)} %get-tuple-element.322, s32[16]{0:T(128)S(1)} %add_add_fusion.2, bf16[256,16,128]{2,1,0:T(8,128)(2,1)} %get-tuple-element.321, s32[]{:T(128)S(6)} %select_n.88), kind=kOutput, calls=%fused_computation.45.clone.1 | convolution fusion | flops 25165824 | bytes 458820 | tf_op jit(solution)/shard_map/while/body/eval_jaxpr/kbc,kcm->kbm/dot_general | solution.py:77
  419.6 8.7 %fusion.88 = f32[16,16,256]{2,1,0:T(8,128)S(1)} fusion(s32[128,256]{1,0:T(8,128)S(1)} %get-tuple-element.322, s32[16]{0:T(128)S(1)} %add_add_fusion.2, bf16[256,16,128]{2,1,0:T(8,128)(2,1)} %get-tuple-element.321, s32[]{:T(128)S(6)} %select_n.88), kind=kOutput, calls=%fused_computation.45.clone.1 | convolution fusion | flops 25165824 | bytes 458820 | tf_op jit(solution)/shard_map/while/body/eval_jaxpr/kbc,kcm->kbm/dot_general | solution.py:77
  454.7 8.7 %fusion.88 = f32[16,16,256]{2,1,0:T(8,128)S(1)} fusion(s32[128,256]{1,0:T(8,128)S(1)} %get-tuple-element.322, s32[16]{0:T(128)S(1)} %add_add_fusion.2, bf16[256,16,128]{2,1,0:T(8,128)(2,1)} %get-tuple-element.321, s32[]{:T(128)S(6)} %select_n.88), kind=kOutput, calls=%fused_computation.45.clone.1 | convolution fusion | flops 25165824 | bytes 458820 | tf_op jit(solution)/shard_map/while/body/eval_jaxpr/kbc,kcm->kbm/dot_general | solution.py:77
  489.8 8.7 %fusion.88 = f32[16,16,256]{2,1,0:T(8,128)S(1)} fusion(s32[128,256]{1,0:T(8,128)S(1)} %get-tuple-element.322, s32[16]{0:T(128)S(1)} %add_add_fusion.2, bf16[256,16,128]{2,1,0:T(8,128)(2,1)} %get-tuple-element.321, s32[]{:T(128)S(6)} %select_n.88), kind=kOutput, calls=%fused_computation.45.clone.1 | convolution fusion | flops 25165824 | bytes 458820 | tf_op jit(solution)/shard_map/while/body/eval_jaxpr/kbc,kcm->kbm/dot_general | solution.py:77
  525.0 8.7 %fusion.88 = f32[16,16,256]{2,1,0:T(8,128)S(1)} fusion(s32[128,256]{1,0:T(8,128)S(1)} %get-tuple-element.322, s32[16]{0:T(128)S(1)} %add_add_fusion.2, bf16[256,16,128]{2,1,0:T(8,128)(2,1)} %get-tuple-element.321, s32[]{:T(128)S(6)} %select_n.88), kind=kOutput, calls=%fused_computation.45.clone.1 | convolution fusion | flops 25165824 | bytes 458820 | tf_op jit(solution)/shard_map/while/body/eval_jaxpr/kbc,kcm->kbm/dot_general | solution.py:77
  560.1 8.7 %fusion.88 = f32[16,16,256]{2,1,0:T(8,128)S(1)} fusion(s32[128,256]{1,0:T(8,128)S(1)} %get-tuple-element.322, s32[16]{0:T(128)S(1)} %add_add_fusion.2, bf16[256,16,128]{2,1,0:T(8,128)(2,1)} %get-tuple-element.321, s32[]{:T(128)S(6)} %select_n.88), kind=kOutput, calls=%fused_computation.45.clone.1 | convolution fusion | flops 25165824 | bytes 458820 | tf_op jit(solution)/shard_map/while/body/eval_jaxpr/kbc,kcm->kbm/dot_general | solution.py:77
  595.2 8.7 %fusion.88 = f32[16,16,256]{2,1,0:T(8,128)S(1)} fusion(s32[128,256]{1,0:T(8,128)S(1)} %get-tuple-element.322, s32[16]{0:T(128)S(1)} %add_add_fusion.2, bf16[256,16,128]{2,1,0:T(8,128)(2,1)} %get-tuple-element.321, s32[]{:T(128)S(6)} %select_n.88), kind=kOutput, calls=%fused_computation.45.clone.1 | convolution fusion | flops 25165824 | bytes 458820 | tf_op jit(solution)/shard_map/while/body/eval_jaxpr/kbc,kcm->kbm/dot_general | solution.py:77
  630.3 8.7 %fusion.88 = f32[16,16,256]{2,1,0:T(8,128)S(1)} fusion(s32[128,256]{1,0:T(8,128)S(1)} %get-tuple-element.322, s32[16]{0:T(128)S(1)} %add_add_fusion.2, bf16[256,16,128]{2,1,0:T(8,128)(2,1)} %get-tuple-element.321, s32[]{:T(128)S(6)} %select_n.88), kind=kOutput, calls=%fused_computation.45.clone.1 | convolution fusion | flops 25165824 | bytes 458820 | tf_op jit(solution)/shard_map/while/body/eval_jaxpr/kbc,kcm->kbm/dot_general | solution.py:77
  665.4 8.7 %fusion.88 = f32[16,16,256]{2,1,0:T(8,128)S(1)} fusion(s32[128,256]{1,0:T(8,128)S(1)} %get-tuple-element.322, s32[16]{0:T(128)S(1)} %add_add_fusion.2, bf16[256,16,128]{2,1,0:T(8,128)(2,1)} %get-tuple-element.321, s32[]{:T(128)S(6)} %select_n.88), kind=kOutput, calls=%fused_computation.45.clone.1 | convolution fusion | flops 25165824 | bytes 458820 | tf_op jit(solution)/shard_map/while/body/eval_jaxpr/kbc,kcm->kbm/dot_general | solution.py:77
  682.8 10.5 %copy.21 = f32[256,2,16,256]{0,2,1,3:T(8,128)} copy(f32[256,2,16,256]{3,2,1,0:T(8,128)} %bitcast.17) | data formatting | bytes 16777216 | tf_op jit(solution)/shard_map/reshape | solution.py:84
  693.3 78.6 %reduce-scatter.2.cloned.1.call-done = f32[256,2,16,64]{0,2,1,3:T(8,128)} async-done(((f32[256,2,16,256]{0,2,1,3:T(8,128)}), f32[256,2,16,64]{0,2,1,3:T(8,128)}) %reduce-scatter.2.cloned.1.call-update) | async-done | bytes 2097168 | tf_op jit(solution)/shard_map/reduce_scatter | solution.py:114
  (142 shorter events, 450.6 us)
Async XLA Ops:
  47.6 11.4 %copy-start = (s32[256,512]{1,0:T(8,128)S(1)}, s32[256,512]{1,0:T(8,128)}, u32[]{:S(2)}) copy-start(s32[256,512]{1,0:T(8,128)} %param.9) | copy-start | bytes 1572868
  47.6 39.6 %all-to-all-start = ((bf16[4,32,16,512]{3,2,0,1:T(8,128)(2,1)}), bf16[4,32,16,512]{3,2,0,1:T(8,128)(2,1)S(1)}, u32[]{:S(2)}, u32[]{:S(2)}) async-start(bf16[4,32,16,512]{3,2,0,1:T(8,128)(2,1)} %copy.17), calls=%async_computation | async-start | bytes 4194304 | tf_op jit(solution)/shard_map/all_to_all | solution.py:109
  58.9 712.9 %reduce-scatter.2.cloned.1.call-start = ((), (), s32[]{:S(2)}) async-start(), calls=%async_computation.2 | async-start | bytes 10485760 | tf_op jit(solution)/shard_map/reduce_scatter | solution.py:114
Sparse Core Ops, SparseCore 0:
  693.4 78.4 reduce-scatter.1
where the time goes:
time: 791 us; the launch traced here: 782 us
  matrix products  545 us (69%)
  waiting for transfers between devices  104 us (13%)
  other arithmetic  37.2 us (5%)
  local copies, waits for them, and re-layouts  35.7 us (5%)
  loops' own time  35.1 us (4%)
  between operations  13.9 us (2%)
  starting transfers between devices  11.4 us (1%)
    dot_general x16, matrix products, one_block(): jnp.einsum('kbc,kcm->kbm', real_piece, sine, preferred_element_type=jnp.f...  139 us
    dot_general x16, matrix products, one_block(): jnp.einsum('kbc,kcm->kbm', real_piece, cosine, preferred_element_type=jnp...  138 us
    dot_general x16, matrix products, one_block(): jnp.einsum('kbc,kcm->kbm', imag_piece, sine, preferred_element_type=jnp.f...  126 us
    dot_general x16, matrix products, one_block(): jnp.einsum('kbc,kcm->kbm', imag_piece, cosine, preferred_element_type=jnp...  125 us
    reduce_scatter x1, waiting for transfers between devices, body(): lax.psum_scatter(partial_spec, 'grp', scatter_dimension=3, tiled=True)  78.6 us
    another operation x1, loops' own time, dedisperse(): blocks = lax.map(one_block, jnp.arange(bins_count // KBLK, dtype=jnp.int32))  32.2 us
    all_to_all x1, waiting for transfers between devices, body(): lax.all_to_all(blocked, 'chan', split_axis=1, concat_axis=0, tiled=True)  25.5 us
  transfers between devices with their start and end apart: 2, of which 2 were waited for; matrix products, arithmetic and copies ran while one was open for 0% of the time, Pallas kernels for 0%

commit v1 on v0

v1 whole, which is shorter than its diff:
```python
import math

import jax
import jax.numpy as jnp
from jax import lax
from jax.experimental import pallas as pl
from jax.experimental.pallas import tpu as pltpu
from jax.sharding import PartitionSpec as P

INTEG = 8
PHASES = 4096
KBLK = 16
CHUNKS = 4
VMEM_LIMIT = 56 * 1024 * 1024


def sin_cos(steps, turn):
    quarter = turn // 4
    steps = steps & (turn - 1)
    quadrant = (steps + quarter // 2) >> (quarter.bit_length() - 1)
    x = (steps - quadrant * quarter).astype(jnp.float32) * jnp.float32(2.0 * math.pi / turn)
    y = x * x
    s = x * (1.0 + y * (-1.0 / 6 + y * (1.0 / 120 + y * (-1.0 / 5040 + y * (1.0 / 362880)))))
    c = 1.0 + y * (-0.5 + y * (1.0 / 24 + y * (-1.0 / 720 + y * (1.0 / 40320))))
    swap = (quadrant & 1) == 1
    sine = jnp.where(swap, c, s)
    cosine = jnp.where(swap, s, c)
    sine = jnp.where((quadrant & 2) == 2, -sine, sine)
    cosine = jnp.where(((quadrant + 1) & 2) == 2, -cosine, cosine)
    return sine, cosine


def detect_kernel(first, delays, volts, out, spread, rows, weights, *, total):
    dishes, beams = delays.shape
    time = volts.shape[1]
    frequency = first[0] + pl.program_id(0) + total
    sine, cosine = sin_cos(delays[...] * frequency, PHASES)
    scale = jnp.float32(1.0 / math.sqrt(dishes))
    real = (cosine * scale).astype(jnp.bfloat16)
    imag = (-(sine * scale)).astype(jnp.bfloat16)
    width = min(beams, 128)
    for n in range(beams // width):
        cols = slice(n * width, (n + 1) * width)
        weights[n, :dishes, :width] = real[:, cols]
        weights[n, :dishes, width:] = imag[:, cols]
        weights[n, dishes:, :width] = -imag[:, cols]
        weights[n, dishes:, width:] = real[:, cols]
    spread[...] = volts[0].astype(jnp.float32)
    blocks, span, _ = rows.shape
    piece = span // INTEG
    for tb in range(blocks):
        for s in range(INTEG):
            rows[tb, s * piece : (s + 1) * piece, :] = spread[
                pl.ds(tb * span + s, piece, stride=INTEG), :
            ].astype(jnp.bfloat16)
    owners, _, held, _ = out.shape
    for n in range(beams // width):
        parts = []
        for tb in range(blocks):
            beam = jnp.dot(rows[tb], weights[n], preferred_element_type=jnp.float32)
            power = beam[:, :width] * beam[:, :width] + beam[:, width:] * beam[:, width:]
            mean = jnp.sum(power.reshape(INTEG, piece, width), axis=0) * jnp.float32(1.0 / INTEG)
            parts.append(mean)
        series = jnp.concatenate(parts, axis=0).T.astype(jnp.bfloat16)
        share = width // held
        out[n * share : (n + 1) * share, 0, :, :] = series.reshape(share, held, time // INTEG)


def detect(voltages, delays, first, total, owners):
    local, time, doubled = voltages.shape
    dishes, beams = delays.shape
    held = beams // owners
    steps = time // INTEG
    blocks = 8
    width = min(beams, 128)
    return pl.pallas_call(
        lambda *refs: detect_kernel(*refs, total=total),
        grid=(local,),
        in_specs=[
            pl.BlockSpec(memory_space=pltpu.SMEM),
            pl.BlockSpec((dishes, beams), lambda i: (0, 0)),
            pl.BlockSpec((1, time, doubled), lambda i: (i, 0, 0)),
        ],
        out_specs=pl.BlockSpec((owners, 1, held, steps), lambda i: (0, i, 0, 0)),
        out_shape=jax.ShapeDtypeStruct((owners, local, held, steps), jnp.bfloat16),
        scratch_shapes=[
            pltpu.VMEM((time, doubled), jnp.float32),
            pltpu.VMEM((blocks, time // blocks, doubled), jnp.bfloat16),
            pltpu.VMEM((beams // width, doubled, 2 * width), jnp.bfloat16),
        ],
        compiler_params=pltpu.CompilerParams(vmem_limit_bytes=VMEM_LIMIT),
        name="detect",
    )(first.reshape(1), delays, voltages)


def spectra_kernel(series, table, out, wide, rows):
    channels, beams, length = series.shape
    bins = length // 2
    planes, _, lanes = wide.shape
    for q in range(planes):
        piece = series[:, :, q * lanes : (q + 1) * lanes]
        wide[q] = piece.reshape(channels * beams, lanes).astype(jnp.float32)
    for b in range(beams):
        mine = jnp.concatenate(
            [wide[q, pl.ds(b, channels, stride=beams), :] for q in range(planes)], axis=1
        ).astype(jnp.bfloat16)
        rows[b * length : (b + 1) * length, :] = lax.dot_general(
            table[...], mine, (((1,), (1,)), ((), ())), preferred_element_type=jnp.float32
        )

    def gather(k, carry):
        real = rows[pl.ds(k, beams, stride=length), :]
        imag = rows[pl.ds(k + bins, beams, stride=length), :]
        out[k] = jnp.concatenate([real, imag], axis=0).astype(jnp.bfloat16)
        return carry

    lax.fori_loop(0, bins, gather, 0, unroll=8)


def spectra(series, table):
    channels, beams, length = series.shape
    return pl.pallas_call(
        spectra_kernel,
        out_shape=jax.ShapeDtypeStruct((length // 2, 2 * beams, channels), jnp.bfloat16),
        scratch_shapes=[
            pltpu.VMEM((length // 128, channels * beams, 128), jnp.float32),
            pltpu.VMEM((beams * length, channels), jnp.float32),
        ],
        compiler_params=pltpu.CompilerParams(vmem_limit_bytes=VMEM_LIMIT),
        name="spectra",
    )(series, table)


def dedisperse_kernel(shifts, spec, keep, send, cosines, sines, *, start, length, scale):
    step = pl.program_id(0)
    beams = spec.shape[1] // 2
    half = keep.shape[2]

    @pl.when(step == 0)
    def _():
        sine, cosine = sin_cos(shifts[...], length)
        cosines[0] = cosine
        sines[0] = sine

        def extend(j, carry):
            s, c = sines[j - 1], cosines[j - 1]
            cosines[j] = c * cosines[0] - s * sines[0]
            sines[j] = s * cosines[0] + c * sines[0]
            return carry

        lax.fori_loop(1, KBLK, extend, 0)

    base_s, base_c = sin_cos(shifts[...] * (start + step * KBLK), length)
    base_s = base_s * scale
    base_c = base_c * scale

    def one(j, carry):
        c, s = cosines[j], sines[j]
        factor = jnp.concatenate(
            [
                (base_c * c - base_s * s).astype(jnp.bfloat16),
                (base_s * c + base_c * s).astype(jnp.bfloat16),
            ],
            axis=0,
        )
        both = spec[j]
        real = both[:beams]
        imag = both[beams:]
        left = jnp.concatenate(
            [jnp.concatenate([real, -imag], axis=1), jnp.concatenate([imag, real], axis=1)], axis=0
        )
        result = jnp.dot(left, factor, preferred_element_type=jnp.float32).astype(jnp.bfloat16)
        keep[j] = result[:, :half]
        send[j] = result[:, half:]
        return carry

    lax.fori_loop(0, KBLK, one, 0, unroll=2)


def dedisperse(shifts, spec, chunk, chunks, scale):
    bins, rows, channels = spec.shape
    trials = shifts.shape[1]
    count = bins // chunks
    steps = count // KBLK
    shape = jax.ShapeDtypeStruct((count, rows, trials // 2), jnp.bfloat16)
    block = pl.BlockSpec((KBLK, rows, trials // 2), lambda i: (i, 0, 0))
    return pl.pallas_call(
        lambda *refs: dedisperse_kernel(*refs, start=chunk * count, length=2 * bins, scale=scale),
        grid=(steps,),
        in_specs=[
            pl.BlockSpec((channels, trials), lambda i: (0, 0)),
            pl.BlockSpec((KBLK, rows, channels), lambda i: (i + chunk * steps, 0, 0)),
        ],
        out_specs=[block, block],
        out_shape=[shape, shape],
        scratch_shapes=[
            pltpu.VMEM((KBLK, channels, trials), jnp.float32),
            pltpu.VMEM((KBLK, channels, trials), jnp.float32),
        ],
        compiler_params=pltpu.CompilerParams(vmem_limit_bytes=VMEM_LIMIT),
        name=f"dedisperse{chunk}",
    )(shifts, spec)


def dft_table(length):
    bins = length // 2
    row = lax.broadcasted_iota(jnp.int32, (length, length), 0)
    sample = lax.broadcasted_iota(jnp.int32, (length, length), 1)
    sine, cosine = sin_cos(sample * ((row & (bins - 1)) + 1), length)
    return (jnp.where(row < bins, cosine, -sine) * jnp.float32(1.0 / math.sqrt(length))).astype(
        jnp.bfloat16
    )


def fold(values):
    half = values.shape[0] // 2
    return jnp.concatenate([values[:half], values[half:]], axis=-1)


def body(voltages, delays, shifts):
    owners = lax.axis_size("chan")
    groups = lax.axis_size("grp")
    local = voltages.shape[0]
    total = local * owners * groups
    group = lax.axis_index("grp")
    first = (lax.axis_index("chan") * groups + group) * local
    detected = detect(voltages, delays, first, total, owners)
    moved = lax.all_to_all(detected, "chan", split_axis=0, concat_axis=0, tiled=True)
    length = moved.shape[3]
    series = moved.reshape(owners * local, moved.shape[2], length)

    trials = shifts.shape[0]
    block = trials // groups
    mine = lax.dynamic_index_in_dim(
        shifts.reshape(trials, owners, groups, local), group, axis=2, keepdims=False
    ).reshape(groups, block, owners * local)
    ordered = [
        lax.dynamic_index_in_dim(mine, group ^ flip, axis=0, keepdims=False) for flip in (0, 2, 1, 3)
    ]
    shifts_t = jnp.concatenate(ordered, axis=0).T

    spec = spectra(series, dft_table(length))
    scale = 1.0 / math.sqrt(total)
    powers = []
    for chunk in range(CHUNKS):
        keep, send = dedisperse(shifts_t, spec, chunk, CHUNKS, scale)
        got = lax.ppermute(send, "grp", [(g, g ^ 1) for g in range(groups)])
        both = keep.astype(jnp.float32) + got.astype(jnp.float32)
        away = fold(both[:, :, block:]).astype(jnp.bfloat16)
        back = lax.ppermute(away, "grp", [(g, g ^ 2) for g in range(groups)])
        whole = fold(both[:, :, :block]) + back.astype(jnp.float32)
        beams = whole.shape[1] // 2
        power = whole[:, :beams] ** 2 + whole[:, beams:] ** 2
        count = power.shape[0]
        powers.append(power.reshape(count, beams, 2, block).transpose(3, 1, 2, 0).reshape(block, beams, 2 * count))
    return jnp.concatenate(powers, axis=2)


def solution(mesh):
    placed = (P(("chan", "grp"), None, None), P(), P())
    return jax.shard_map(
        body, mesh=mesh, in_specs=placed, out_specs=P("grp", "chan", None), check_vma=False
    )
```

time: 791 us -> 142 us (0.18); the launches traced: 782 us -> 141 us
  matrix products: 545 us -> 0 us
  Pallas kernels: 0 us -> 64.3 us
  waiting for transfers between devices: 104 us -> 42 us
  loops' own time: 35.1 us -> 0 us
  other arithmetic: 37.2 us -> 7.76 us
  local copies, waits for them, and re-layouts: 35.7 us -> 9.19 us
  between operations: 13.9 us -> 0.35 us
    dot_general x69 -> x0, matrix products: 545 us -> none  [the longest x16 139 us: one_block(): jnp.einsum('kbc,kcm->kbm', real_piece, sine, preferred_element_type=jnp.f...]
    reduce_scatter x1 -> x0, waiting for transfers between devices: 78.6 us -> none  [body(): lax.psum_scatter(partial_spec, 'grp', scatter_dimension=3, tiled=True)]
    pallas_call x0 -> x6, Pallas kernels: none -> 64.3 us  [the longest x4 43.3 us: dedisperse(): pl.pallas_call(lambda *refs: dedisperse_kernel(*refs, start=chunk * count...]
    another operation x2 -> x0, loops' own time: 35.1 us -> none  [the longest x1 32.2 us: dedisperse(): blocks = lax.map(one_block, jnp.arange(bins_count // KBLK, dtype=jnp.int32))]
    ppermute x0 -> x8, waiting for transfers between devices: none -> 17.8 us  [the longest x4 17.8 us: body(): back = lax.ppermute(away, 'grp', [(g, g ^ 2) for g in range(groups)])]
    dynamic_update_slice x16 -> x0, other arithmetic: 13.5 us -> none  [dedisperse(): blocks = lax.map(one_block, jnp.arange(bins_count // KBLK, dtype=jnp.int32))]
    dynamic_slice x21 -> x2, local copies, waits for them, and re-layouts: 12.9 us -> 0.26 us  [the longest x1 0.23 us: body(): lax.dynamic_index_in_dim(mine, group ^ flip, axis=0, keepdims=False)]
    reduce_sum x4 -> x0, other arithmetic: 12.3 us -> none  [detect(): jnp.sum(intensity.reshape(steps_count, INTEG, half_width), axis=1)]
  transfers between devices with their start and end apart: 2 -> 9, of which waited for: 2 -> 4; matrix products, arithmetic and copies ran while one was open for 0% -> 7% of each run, Pallas kernels for 0% -> 23%
where the time goes in v1:
time: 142 us; the launch traced here: 141 us
  Pallas kernels  64.3 us (45%)
  waiting for transfers between devices  42 us (30%)
  starting transfers between devices  17.6 us (12%)
  local copies, waits for them, and re-layouts  9.19 us (6%)
  other arithmetic  7.76 us (5%)
    pallas_call x4, Pallas kernels, dedisperse(): pl.pallas_call(lambda *refs: dedisperse_kernel(*refs, start=chunk * count...  43.3 us
    all_to_all x1, waiting for transfers between devices, body(): lax.all_to_all(detected, 'chan', split_axis=0, concat_axis=0, tiled=True)  24.2 us
    ppermute x4, waiting for transfers between devices, body(): back = lax.ppermute(away, 'grp', [(g, g ^ 2) for g in range(groups)])  17.8 us
    pallas_call x1, Pallas kernels, detect(): pl.pallas_call(lambda *refs: detect_kernel(*refs, total=total), grid=(loc...  12.9 us
    all_to_all x1, starting transfers between devices, body(): lax.all_to_all(detected, 'chan', split_axis=0, concat_axis=0, tiled=True)  11.3 us
    pallas_call x1, Pallas kernels, spectra(): pl.pallas_call(spectra_kernel, out_shape=jax.ShapeDtypeStruct((length //...  8.16 us
    ppermute x4, starting transfers between devices, body(): back = lax.ppermute(away, 'grp', [(g, g ^ 2) for g in range(groups)])  3.43 us
    reshape x8, local copies, waits for them, and re-layouts, body(): power.reshape(count, beams, 2, block).transpose(3, 1, 2, 0)  3.31 us
  transfers between devices with their start and end apart: 9, of which 4 were waited for; matrix products, arithmetic and copies ran while one was open for 7% of the time, Pallas kernels for 23%

profile of v1, /device:TPU:1, one launch (start us, length us, event | category | flops | bytes accessed | tf_op | source)
XLA Modules:
  0.0 141.1 jit_solution(10585242415797446827)
XLA Ops:
  0.0 12.9 %detect.1 = bf16[32,4,16,512]{3,2,1,0:T(8,128)(2,1)} custom-call(s32[1]{0:T(128)} %bitcast.5.refs_0_, s32[64,512]{1,0:T(8,128)} %refs_1_.1, bf16[4,4096,128]{2,1,0:T(8,128)(2,1)} %refs_2_.1), custom_call_target="tpu_custom_call" | custom-call | tf_op jit(solution)/shard_map/detect/pallas_call | solution.py:76
  12.9 11.3 %all-to-all-start = ((bf16[32,4,16,512]{3,2,1,0:T(8,128)(2,1)}), bf16[32,4,16,512]{3,2,1,0:T(8,128)(2,1)S(1)}, u32[]{:S(2)}, u32[]{:S(2)}) async-start(bf16[32,4,16,512]{3,2,1,0:T(8,128)(2,1)} %detect.1), calls=%async_computation | async-start | bytes 4194304 | tf_op jit(solution)/shard_map/all_to_all | solution.py:228
  25.1 0.8 add_bitcast_fusion.refs_0_
  25.8 2.4 %fusion.2.table = bf16[512,512]{1,0:T(8,128)(2,1)} fusion(s32[512]{0:T(512)S(1)} %fusion.11, pred[512]{0:T(512)(128)(4,1)S(1)} %iota_compare_fusion), kind=kLoop, calls=%fused_computation.5 | loop fusion | flops 11272192 | bytes 526848 | tf_op jit(solution)/shard_map/convert_element_type | solution.py:210
  28.3 24.2 %all-to-all-done = bf16[32,4,16,512]{3,2,1,0:T(8,128)(2,1)S(1)} async-done(((bf16[32,4,16,512]{3,2,1,0:T(8,128)(2,1)}), bf16[32,4,16,512]{3,2,1,0:T(8,128)(2,1)S(1)}, u32[]{:S(2)}, u32[]{:S(2)}) %all-to-all-start) | async-done | bytes 2097184 | tf_op jit(solution)/shard_map/all_to_all | solution.py:228
  52.5 1.3 copy-done
  53.8 8.2 %spectra.1.refs_1_ = bf16[256,32,128]{2,1,0:T(8,128)(2,1)} custom-call(bf16[128,16,512]{2,1,0:T(8,128)(2,1)} %bitcast.24, bf16[512,512]{1,0:T(8,128)(2,1)} %fusion.2.table), custom_call_target="tpu_custom_call" | custom-call | tf_op jit(solution)/shard_map/spectra/pallas_call | solution.py:122
  62.0 10.8 %dedisperse3.1 = (bf16[64,32,128]{2,1,0:T(8,128)(2,1)}, bf16[64,32,128]{2,1,0:T(8,128)(2,1)}) custom-call(s32[128,256]{1,0:T(8,128)} %add_bitcast_fusion.refs_0_, bf16[256,32,128]{2,1,0:T(8,128)(2,1)} %spectra.1.refs_1_), custom_call_target="tpu_custom_call" | custom-call | tf_op jit(solution)/shard_map/dedisperse3/pallas_call | solution.py:187
  72.8 2.2 %collective-permute-start.6 = (bf16[64,32,128]{2,1,0:T(8,128)(2,1)}, bf16[64,32,128]{2,1,0:T(8,128)(2,1)S(1)}, u32[]{:S(2)}, u32[]{:S(2)}) collective-permute-start(bf16[64,32,128]{2,1,0:T(8,128)(2,1)} %get-tuple-element.20), channel_id=1, source_target_pairs={{0,1},{1,0},{2,3},{3,2},{4,5},{5,4},{6,7},{7,6},{8,9},{9,8},{10,11... | collective-permute-start | bytes 1572872 | tf_op jit(solution)/shard_map/ppermute | solution.py:247
  75.0 10.8 %dedisperse2.1 = (bf16[64,32,128]{2,1,0:T(8,128)(2,1)}, bf16[64,32,128]{2,1,0:T(8,128)(2,1)}) custom-call(s32[128,256]{1,0:T(8,128)} %add_bitcast_fusion.refs_0_, bf16[256,32,128]{2,1,0:T(8,128)(2,1)} %spectra.1.refs_1_), custom_call_target="tpu_custom_call" | custom-call | tf_op jit(solution)/shard_map/dedisperse2/pallas_call | solution.py:187
  85.8 10.9 %dedisperse1.1 = (bf16[64,32,128]{2,1,0:T(8,128)(2,1)}, bf16[64,32,128]{2,1,0:T(8,128)(2,1)}) custom-call(s32[128,256]{1,0:T(8,128)} %add_bitcast_fusion.refs_0_, bf16[256,32,128]{2,1,0:T(8,128)(2,1)} %spectra.1.refs_1_), custom_call_target="tpu_custom_call" | custom-call | tf_op jit(solution)/shard_map/dedisperse1/pallas_call | solution.py:187
  96.7 10.8 %dedisperse0.1 = (bf16[64,32,128]{2,1,0:T(8,128)(2,1)}, bf16[64,32,128]{2,1,0:T(8,128)(2,1)}) custom-call(s32[128,256]{1,0:T(8,128)} %add_bitcast_fusion.refs_0_, bf16[256,32,128]{2,1,0:T(8,128)(2,1)} %spectra.1.refs_1_), custom_call_target="tpu_custom_call" | custom-call | tf_op jit(solution)/shard_map/dedisperse0/pallas_call | solution.py:187
  108.7 1.0 collective-permute-start.7
  110.3 0.8 collective-permute-start.5
  111.7 0.8 collective-permute-start.3
  112.6 0.9 copy-done.1
  114.1 0.8 collective-permute-start.1
  115.1 1.4 collective-permute-done.7
  116.7 5.4 %collective-permute-done.5 = bf16[32,32,128]{2,1,0:T(8,128)(2,1)S(1)} collective-permute-done((bf16[32,32,128]{2,1,0:T(8,128)(2,1)S(1)}, bf16[32,32,128]{2,1,0:T(8,128)(2,1)S(1)}, u32[]{:S(2)}, u32[]{:S(2)}) %collective-permute-start.5) | collective-permute-done | bytes 262176 | tf_op jit(solution)/shard_map/ppermute | solution.py:250
  122.2 11.0 %collective-permute-done.1 = bf16[32,32,128]{2,1,0:T(8,128)(2,1)S(1)} collective-permute-done((bf16[32,32,128]{2,1,0:T(8,128)(2,1)S(1)}, bf16[32,32,128]{2,1,0:T(8,128)(2,1)S(1)}, u32[]{:S(2)}, u32[]{:S(2)}) %collective-permute-start.1) | collective-permute-done | bytes 262176 | tf_op jit(solution)/shard_map/ppermute | solution.py:250
  135.2 1.1 copy.9
  136.3 1.2 maximum_add_fusion.1
  138.1 1.2 pad_maximum_fusion
  139.4 1.8 %copy.13 = f32[64,16,256]{2,1,0:T(8,128)} copy(f32[64,16,256]{0,2,1:T(8,128)S(1)} %pad_maximum_fusion) | data formatting | bytes 2097152 | tf_op jit(solution)/shard_map/concatenate | solution.py:256
  (59 shorter events, 6.9 us)
Async XLA Ops:
  12.9 11.3 %copy-start.5 = (s32[256,512]{1,0:T(8,128)S(1)}, s32[256,512]{1,0:T(8,128)}, u32[]{:S(2)}) copy-start(s32[256,512]{1,0:T(8,128)} %param.5) | copy-start | bytes 1572868
  12.9 39.6 %all-to-all-start = ((bf16[32,4,16,512]{3,2,1,0:T(8,128)(2,1)}), bf16[32,4,16,512]{3,2,1,0:T(8,128)(2,1)S(1)}, u32[]{:S(2)}, u32[]{:S(2)}) async-start(bf16[32,4,16,512]{3,2,1,0:T(8,128)(2,1)} %detect.1), calls=%async_computation | async-start | bytes 4194304 | tf_op jit(solution)/shard_map/all_to_all | solution.py:228
  52.5 1.3 copy-start
  72.8 35.3 %collective-permute-start.6 = (bf16[64,32,128]{2,1,0:T(8,128)(2,1)}, bf16[64,32,128]{2,1,0:T(8,128)(2,1)S(1)}, u32[]{:S(2)}, u32[]{:S(2)}) collective-permute-start(bf16[64,32,128]{2,1,0:T(8,128)(2,1)} %get-tuple-element.20), channel_id=1, source_target_pairs={{0,1},{1,0},{2,3},{3,2},{4,5},{5,4},{6,7},{7,6},{8,9},{9,8},{10,11... | collective-permute-start | bytes 1572872 | tf_op jit(solution)/shard_map/ppermute | solution.py:247
  85.8 21.7 %copy-start.7 = (bf16[64,32,128]{2,1,0:T(8,128)(2,1)S(1)}, bf16[64,32,128]{2,1,0:T(8,128)(2,1)}, u32[]{:S(2)}) copy-start(bf16[64,32,128]{2,1,0:T(8,128)(2,1)} %get-tuple-element.18) | copy-start | bytes 1572868
  85.8 22.3 %copy-start.4 = (bf16[64,32,128]{2,1,0:T(8,128)(2,1)S(1)}, bf16[64,32,128]{2,1,0:T(8,128)(2,1)}, u32[]{:S(2)}) copy-start(bf16[64,32,128]{2,1,0:T(8,128)(2,1)} %get-tuple-element.19) | copy-start | bytes 1572868
  96.7 10.9 %copy-start.6 = (bf16[64,32,128]{2,1,0:T(8,128)(2,1)S(1)}, bf16[64,32,128]{2,1,0:T(8,128)(2,1)}, u32[]{:S(2)}) copy-start(bf16[64,32,128]{2,1,0:T(8,128)(2,1)} %get-tuple-element.16) | copy-start | bytes 1572868
  107.5 2.2 %collective-permute-start.4 = (bf16[64,32,128]{2,1,0:T(8,128)(2,1)S(1)}, bf16[64,32,128]{2,1,0:T(8,128)(2,1)S(1)}, u32[]{:S(2)}, u32[]{:S(2)}) collective-permute-start(bf16[64,32,128]{2,1,0:T(8,128)(2,1)S(1)} %copy-done.7), channel_id=1, source_target_pairs={{0,1},{1,0},{2,3},{3,2},{4,5},{5,4},{6,7},{7,6},{8,9},{9,8},{10,11... | collective-permute-start | bytes 1572872 | tf_op jit(solution)/shard_map/ppermute | solution.py:247
  107.5 3.6 %collective-permute-start.2 = (bf16[64,32,128]{2,1,0:T(8,128)(2,1)S(1)}, bf16[64,32,128]{2,1,0:T(8,128)(2,1)S(1)}, u32[]{:S(2)}, u32[]{:S(2)}) collective-permute-start(bf16[64,32,128]{2,1,0:T(8,128)(2,1)S(1)} %copy-done.6), channel_id=1, source_target_pairs={{0,1},{1,0},{2,3},{3,2},{4,5},{5,4},{6,7},{7,6},{8,9},{9,8},{10,11... | collective-permute-start | bytes 1572872 | tf_op jit(solution)/shard_map/ppermute | solution.py:247
  108.0 4.6 %collective-permute-start = (bf16[64,32,128]{2,1,0:T(8,128)(2,1)}, bf16[64,32,128]{2,1,0:T(8,128)(2,1)S(1)}, u32[]{:S(2)}, u32[]{:S(2)}) collective-permute-start(bf16[64,32,128]{2,1,0:T(8,128)(2,1)} %get-tuple-element.14), channel_id=1, source_target_pairs={{0,1},{1,0},{2,3},{3,2},{4,5},{5,4},{6,7},{7,6},{8,9},{9,8},{10,11... | collective-permute-start | bytes 1572872 | tf_op jit(solution)/shard_map/ppermute | solution.py:247
  108.1 1.6 %copy-start.3 = (bf16[64,32,128]{2,1,0:T(8,128)(2,1)S(1)}, bf16[64,32,128]{2,1,0:T(8,128)(2,1)}, u32[]{:S(2)}) copy-start(bf16[64,32,128]{2,1,0:T(8,128)(2,1)} %get-tuple-element.17) | copy-start | bytes 1572868
  108.7 7.7 %collective-permute-start.7 = (bf16[32,32,128]{2,1,0:T(8,128)(2,1)S(1)}, bf16[32,32,128]{2,1,0:T(8,128)(2,1)S(1)}, u32[]{:S(2)}, u32[]{:S(2)}) collective-permute-start(bf16[32,32,128]{2,1,0:T(8,128)(2,1)S(1)} %pad_maximum_fusion.4), channel_id=1, source_target_pairs={{0,2},{1,3},{2,0},{3,1},{4,6},{5,7},{6,4},{7,5},{8,10},{9,11},{10,... | collective-permute-start | bytes 786440 | tf_op jit(solution)/shard_map/ppermute | solution.py:250
  109.7 1.4 copy-start.2
  110.3 11.8 %collective-permute-start.5 = (bf16[32,32,128]{2,1,0:T(8,128)(2,1)S(1)}, bf16[32,32,128]{2,1,0:T(8,128)(2,1)S(1)}, u32[]{:S(2)}, u32[]{:S(2)}) collective-permute-start(bf16[32,32,128]{2,1,0:T(8,128)(2,1)S(1)} %pad_maximum_fusion.3), channel_id=1, source_target_pairs={{0,2},{1,3},{2,0},{3,1},{4,6},{5,7},{6,4},{7,5},{8,10},{9,11},{10,... | collective-permute-start | bytes 786440 | tf_op jit(solution)/shard_map/ppermute | solution.py:250
  111.7 24.6 %collective-permute-start.3 = (bf16[32,32,128]{2,1,0:T(8,128)(2,1)S(1)}, bf16[32,32,128]{2,1,0:T(8,128)(2,1)}, u32[]{:S(2)}, u32[]{:S(2)}) collective-permute-start(bf16[32,32,128]{2,1,0:T(8,128)(2,1)S(1)} %pad_maximum_fusion.2), channel_id=1, source_target_pairs={{0,2},{1,3},{2,0},{3,1},{4,6},{5,7},{6,4},{7,5},{8,10},{9,11},{10,... | collective-permute-start | bytes 786440 | tf_op jit(solution)/shard_map/ppermute | solution.py:250
  112.5 1.0 copy-start.1
  114.1 19.2 %collective-permute-start.1 = (bf16[32,32,128]{2,1,0:T(8,128)(2,1)S(1)}, bf16[32,32,128]{2,1,0:T(8,128)(2,1)S(1)}, u32[]{:S(2)}, u32[]{:S(2)}) collective-permute-start(bf16[32,32,128]{2,1,0:T(8,128)(2,1)S(1)} %pad_maximum_fusion.1), channel_id=1, source_target_pairs={{0,2},{1,3},{2,0},{3,1},{4,6},{5,7},{6,4},{7,5},{8,10},{9,11},{10,... | collective-permute-start | bytes 786440 | tf_op jit(solution)/shard_map/ppermute | solution.py:250

commit v2 on v1

v2 whole, which is shorter than its diff:
```python
import math

import jax
import jax.numpy as jnp
from jax import lax
from jax.experimental import pallas as pl
from jax.experimental.pallas import tpu as pltpu
from jax.sharding import PartitionSpec as P

INTEG = 8
PHASES = 4096
KBLK = 16
UNITS = (2, 2, 2, 2)
HALVES = 2
VMEM_LIMIT = 56 * 1024 * 1024


def sin_cos(steps, turn):
    quarter = turn // 4
    steps = steps & (turn - 1)
    quadrant = (steps + quarter // 2) >> (quarter.bit_length() - 1)
    x = (steps - quadrant * quarter).astype(jnp.float32) * jnp.float32(2.0 * math.pi / turn)
    y = x * x
    s = x * (1.0 + y * (-1.0 / 6 + y * (1.0 / 120 + y * (-1.0 / 5040 + y * (1.0 / 362880)))))
    c = 1.0 + y * (-0.5 + y * (1.0 / 24 + y * (-1.0 / 720 + y * (1.0 / 40320))))
    swap = (quadrant & 1) == 1
    sine = jnp.where(swap, c, s)
    cosine = jnp.where(swap, s, c)
    sine = jnp.where((quadrant & 2) == 2, -sine, sine)
    cosine = jnp.where(((quadrant + 1) & 2) == 2, -cosine, cosine)
    return sine, cosine


def detect_kernel(first, delays, volts, out, spread, rows, weights, *, total):
    dishes, beams = delays.shape
    time = volts.shape[1]
    frequency = first[0] + pl.program_id(0) + total
    sine, cosine = sin_cos(delays[...] * frequency, PHASES)
    scale = jnp.float32(1.0 / math.sqrt(dishes))
    real = (cosine * scale).astype(jnp.bfloat16)
    imag = (-(sine * scale)).astype(jnp.bfloat16)
    width = min(beams, 128)
    for n in range(beams // width):
        cols = slice(n * width, (n + 1) * width)
        weights[n, :dishes, :width] = real[:, cols]
        weights[n, :dishes, width:] = imag[:, cols]
        weights[n, dishes:, :width] = -imag[:, cols]
        weights[n, dishes:, width:] = real[:, cols]
    spread[...] = volts[0].astype(jnp.float32)
    blocks, span, _ = rows.shape
    piece = span // INTEG
    for tb in range(blocks):
        for s in range(INTEG):
            rows[tb, s * piece : (s + 1) * piece, :] = spread[
                pl.ds(tb * span + s, piece, stride=INTEG), :
            ].astype(jnp.bfloat16)
    owners, _, held, _ = out.shape
    for n in range(beams // width):
        parts = []
        for tb in range(blocks):
            beam = jnp.dot(rows[tb], weights[n], preferred_element_type=jnp.float32)
            power = beam[:, :width] * beam[:, :width] + beam[:, width:] * beam[:, width:]
            mean = jnp.sum(power.reshape(INTEG, piece, width), axis=0) * jnp.float32(1.0 / INTEG)
            parts.append(mean)
        series = jnp.concatenate(parts, axis=0).T.astype(jnp.bfloat16)
        share = width // held
        out[n * share : (n + 1) * share, 0, :, :] = series.reshape(share, held, time // INTEG)


def detect(voltages, delays, first, total, owners, part):
    local, time, doubled = voltages.shape
    time = time // HALVES
    dishes, beams = delays.shape
    held = beams // owners
    steps = time // INTEG
    blocks = 4
    width = min(beams, 128)
    return pl.pallas_call(
        lambda *refs: detect_kernel(*refs, total=total),
        grid=(local,),
        in_specs=[
            pl.BlockSpec(memory_space=pltpu.SMEM),
            pl.BlockSpec((dishes, beams), lambda i: (0, 0)),
            pl.BlockSpec((1, time, doubled), lambda i: (i, part, 0)),
        ],
        out_specs=pl.BlockSpec((owners, 1, held, steps), lambda i: (0, i, 0, 0)),
        out_shape=jax.ShapeDtypeStruct((owners, local, held, steps), jnp.bfloat16),
        scratch_shapes=[
            pltpu.VMEM((time, doubled), jnp.float32),
            pltpu.VMEM((blocks, time // blocks, doubled), jnp.bfloat16),
            pltpu.VMEM((beams // width, doubled, 2 * width), jnp.bfloat16),
        ],
        compiler_params=pltpu.CompilerParams(vmem_limit_bytes=VMEM_LIMIT),
        name=f"detect{part}",
    )(first.reshape(1), delays, voltages)


def transform_rows(series, table, wide):
    channels, beams, _ = series.shape
    planes, _, lanes = wide.shape
    for q in range(planes):
        piece = series[:, :, q * lanes : (q + 1) * lanes]
        wide[q] = piece.reshape(channels * beams, lanes).astype(jnp.float32)
    for b in range(beams):
        mine = jnp.concatenate(
            [wide[q, pl.ds(b, channels, stride=beams), :] for q in range(planes)], axis=1
        ).astype(jnp.bfloat16)
        yield b, lax.dot_general(
            table[...], mine, (((1,), (1,)), ((), ())), preferred_element_type=jnp.float32
        )


def spectra_start_kernel(series, table, out, wide):
    length = table.shape[0]
    for b, product in transform_rows(series, table, wide):
        out[b * length : (b + 1) * length, :] = product


def spectra_end_kernel(series, table, begun, out, wide, rows):
    beams = series.shape[1]
    length = table.shape[0]
    bins = length // 2
    for b, product in transform_rows(series, table, wide):
        span = slice(b * length, (b + 1) * length)
        rows[span, :] = begun[span, :] + product

    def gather(k, carry):
        real = rows[pl.ds(k, beams, stride=length), :]
        imag = rows[pl.ds(k + bins, beams, stride=length), :]
        out[k] = jnp.concatenate([real, imag], axis=0).astype(jnp.bfloat16)
        return carry

    lax.fori_loop(0, bins, gather, 0, unroll=16)


def spectra(series, table, begun=None):
    channels, beams, steps = series.shape
    length = table.shape[0]
    wide = pltpu.VMEM((steps // 128, channels * beams, 128), jnp.float32)
    params = pltpu.CompilerParams(vmem_limit_bytes=VMEM_LIMIT)
    if begun is None:
        return pl.pallas_call(
            spectra_start_kernel,
            out_shape=jax.ShapeDtypeStruct((beams * length, channels), jnp.float32),
            scratch_shapes=[wide],
            compiler_params=params,
            name="spectra_start",
        )(series, table)
    return pl.pallas_call(
        spectra_end_kernel,
        out_shape=jax.ShapeDtypeStruct((length // 2, 2 * beams, channels), jnp.bfloat16),
        scratch_shapes=[wide, pltpu.VMEM((beams * length, channels), jnp.float32)],
        compiler_params=params,
        name="spectra_end",
    )(series, table, begun)


def factors_kernel(shifts, out, cosines, sines, base_c, base_s, *, length, scale):
    step = pl.program_id(0)
    channels = shifts.shape[0]

    @pl.when(step == 0)
    def _():
        sine, cosine = sin_cos(shifts[...], length)
        cosines[0] = cosine
        sines[0] = sine

        def extend(j, carry):
            s, c = sines[j - 1], cosines[j - 1]
            cosines[j] = c * cosines[0] - s * sines[0]
            sines[j] = s * cosines[0] + c * sines[0]
            return carry

        lax.fori_loop(1, KBLK, extend, 0)

    sine, cosine = sin_cos(shifts[...] * (step * KBLK), length)
    base_s[...] = sine * scale
    base_c[...] = cosine * scale
    tile = min(16, channels)

    def one(r, carry):
        at = pl.ds(pl.multiple_of(r * tile, tile), tile)
        below = pl.ds(pl.multiple_of(channels + r * tile, tile), tile)
        bc = base_c[at, :]
        bs = base_s[at, :]
        for j in range(KBLK):
            c = cosines[j, at, :]
            s = sines[j, at, :]
            out[j, at, :] = (bc * c - bs * s).astype(jnp.bfloat16)
            out[j, below, :] = (bs * c + bc * s).astype(jnp.bfloat16)
        return carry

    lax.fori_loop(0, channels // tile, one, 0)


def dedispersion_factors(shifts, length, scale):
    channels, trials = shifts.shape
    bins = length // 2
    return pl.pallas_call(
        lambda *refs: factors_kernel(*refs, length=length, scale=scale),
        grid=(bins // KBLK,),
        in_specs=[pl.BlockSpec((channels, trials), lambda i: (0, 0))],
        out_specs=pl.BlockSpec((KBLK, 2 * channels, trials), lambda i: (i, 0, 0)),
        out_shape=jax.ShapeDtypeStruct((bins, 2 * channels, trials), jnp.bfloat16),
        scratch_shapes=[
            pltpu.VMEM((KBLK, channels, trials), jnp.float32),
            pltpu.VMEM((KBLK, channels, trials), jnp.float32),
            pltpu.VMEM((channels, trials), jnp.float32),
            pltpu.VMEM((channels, trials), jnp.float32),
        ],
        compiler_params=pltpu.CompilerParams(vmem_limit_bytes=VMEM_LIMIT),
        name="factors",
    )(shifts)


def dedisperse_kernel(factors, spec, keep, send):
    beams = spec.shape[1] // 2
    half = keep.shape[2]
    for j in range(KBLK):
        both = spec[j]
        real = both[:beams]
        imag = both[beams:]
        left = jnp.concatenate(
            [jnp.concatenate([real, -imag], axis=1), jnp.concatenate([imag, real], axis=1)], axis=0
        )
        result = jnp.dot(left, factors[j], preferred_element_type=jnp.float32).astype(jnp.bfloat16)
        keep[j] = result[:, :half]
        send[j] = result[:, half:]


def dedisperse(factors, spec, start, units):
    bins, rows, channels = spec.shape
    trials = factors.shape[2]
    middle = bins // (2 * KBLK)
    shape = jax.ShapeDtypeStruct((2 * units * KBLK, rows, trials // 2), jnp.bfloat16)
    block = pl.BlockSpec((KBLK, rows, trials // 2), lambda i: (i, 0, 0))

    def pick(i):
        return (jnp.where(i < units, start + i, middle + start + i - units), 0, 0)

    return pl.pallas_call(
        dedisperse_kernel,
        grid=(2 * units,),
        in_specs=[
            pl.BlockSpec((KBLK, 2 * channels, trials), pick),
            pl.BlockSpec((KBLK, rows, channels), pick),
        ],
        out_specs=[block, block],
        out_shape=[shape, shape],
        compiler_params=pltpu.CompilerParams(vmem_limit_bytes=VMEM_LIMIT),
        name=f"dedisperse{start}",
    )(factors, spec)


def join_kernel(keep, got, own, away):
    count, rows, lanes = own.shape
    both = keep[...].astype(jnp.float32) + got[...].astype(jnp.float32)
    low = both[:count].reshape(count * rows, lanes)
    high = both[count:].reshape(count * rows, lanes)
    near = lax.broadcasted_iota(jnp.int32, low.shape, 1) < lanes // 2
    own[...] = jnp.where(near, low, pltpu.roll(high, lanes // 2, 1)).reshape(own.shape)
    other = jnp.where(near, pltpu.roll(low, lanes // 2, 1), high)
    away[...] = other.astype(jnp.bfloat16).reshape(away.shape)


def join(keep, got, start):
    count, rows, lanes = keep.shape
    return pl.pallas_call(
        join_kernel,
        out_shape=[
            jax.ShapeDtypeStruct((count // 2, rows, lanes), jnp.float32),
            jax.ShapeDtypeStruct((count // 2, rows, lanes), jnp.bfloat16),
        ],
        compiler_params=pltpu.CompilerParams(vmem_limit_bytes=VMEM_LIMIT),
        name=f"join{start}",
    )(keep, got)


def power_kernel(*refs, pieces):
    owns = refs[:pieces]
    backs = refs[pieces : 2 * pieces]
    out, powers, turned = refs[2 * pieces :]
    block, beams, _ = out.shape
    lanes = powers.shape[1]
    at = 0
    for own, back in zip(owns, backs):
        whole = own[...] + back[...].astype(jnp.float32)
        real = whole[:, :beams]
        imag = whole[:, beams:]
        power = real * real + imag * imag
        rows = power.shape[0] * beams
        powers[at : at + rows, :] = power.reshape(rows, lanes)
        at += rows
    count = at // beams
    for b in range(beams):
        flipped = powers[pl.ds(b, count, stride=beams), :].T
        turned[0, b * block : (b + 1) * block, :] = flipped[:block]
        turned[1, b * block : (b + 1) * block, :] = flipped[block:]
    for m in range(block):
        out[m, :, :count] = turned[0, pl.ds(m, beams, stride=block), :]
        out[m, :, count:] = turned[1, pl.ds(m, beams, stride=block), :]


def final_power(owns, backs):
    beams = owns[0].shape[1] // 2
    lanes = owns[0].shape[2]
    count = sum(own.shape[0] for own in owns)
    block = lanes // 2
    return pl.pallas_call(
        lambda *refs: power_kernel(*refs, pieces=len(owns)),
        out_shape=jax.ShapeDtypeStruct((block, beams, 2 * count), jnp.float32),
        scratch_shapes=[
            pltpu.VMEM((count * beams, lanes), jnp.float32),
            pltpu.VMEM((2, beams * block, count), jnp.float32),
        ],
        compiler_params=pltpu.CompilerParams(vmem_limit_bytes=VMEM_LIMIT),
        name="power",
    )(*owns, *backs)


def dft_table(length):
    bins = length // 2
    row = lax.broadcasted_iota(jnp.int32, (length, length), 0)
    sample = lax.broadcasted_iota(jnp.int32, (length, length), 1)
    sine, cosine = sin_cos(sample * ((row & (bins - 1)) + 1), length)
    return (jnp.where(row < bins, cosine, -sine) * jnp.float32(1.0 / math.sqrt(length))).astype(
        jnp.bfloat16
    )


def body(voltages, delays, shifts):
    owners = lax.axis_size("chan")
    groups = lax.axis_size("grp")
    local = voltages.shape[0]
    total = local * owners * groups
    group = lax.axis_index("grp")
    first = (lax.axis_index("chan") * groups + group) * local
    length = voltages.shape[1] // INTEG
    steps = length // HALVES

    series = []
    for part in range(HALVES):
        detected = detect(voltages, delays, first, total, owners, part)
        moved = lax.all_to_all(detected, "chan", split_axis=0, concat_axis=0, tiled=True)
        series.append(moved.reshape(owners * local, moved.shape[2], steps))

    trials = shifts.shape[0]
    block = trials // groups
    mine = lax.dynamic_index_in_dim(
        shifts.reshape(trials, owners, groups, local), group, axis=2, keepdims=False
    ).reshape(groups, block, owners * local)
    ordered = [
        lax.dynamic_index_in_dim(mine, group ^ flip, axis=0, keepdims=False) for flip in (0, 2, 1, 3)
    ]
    shifts_t = jnp.concatenate(ordered, axis=0).T
    factors = dedispersion_factors(shifts_t, length, 1.0 / math.sqrt(total))

    table = dft_table(length)
    begun = spectra(series[0], table[:, :steps])
    spec = spectra(series[1], table[:, steps:], begun)

    owns, backs, sends = [], [], []
    start = 0
    for turn, units in enumerate(UNITS):
        if turn >= 2:
            spec, sends[turn - 2] = lax.optimization_barrier((spec, sends[turn - 2]))
        keep, send = dedisperse(factors, spec, start, units)
        got = lax.ppermute(send, "grp", [(g, g ^ 1) for g in range(groups)])
        own, away = join(keep, got, start)
        owns.append(own)
        sends.append(away)
        start += units
    for away in sends:
        backs.append(lax.ppermute(away, "grp", [(g, g ^ 2) for g in range(groups)]))
    return final_power(owns, backs)


def solution(mesh):
    placed = (P(("chan", "grp"), None, None), P(), P())
    return jax.shard_map(
        body, mesh=mesh, in_specs=placed, out_specs=P("grp", "chan", None), check_vma=False
    )
```

time: 142 us -> 139 us (0.979)
  Pallas kernels: 64.3 us -> 83.7 us
  waiting for transfers between devices: 42 us -> 23 us
  other arithmetic: 7.76 us -> 2.59 us
  starting transfers between devices: 17.6 us -> 22.3 us
  local copies, waits for them, and re-layouts: 9.19 us -> 6.5 us
    pallas_call x5 -> x12, Pallas kernels: 51.4 us -> 68.2 us  [the longest x4 23.2 us: dedisperse(): pl.pallas_call(dedisperse_kernel, grid=(2 * units,), in_specs=[pl.BlockSp...]
    all_to_all x1 -> x2, waiting for transfers between devices: 24.2 us -> 7.87 us  [body(): lax.all_to_all(detected, 'chan', split_axis=0, concat_axis=0, tiled=True)]
    all_to_all x1 -> x2, starting transfers between devices: 11.3 us -> 17.3 us  [body(): lax.all_to_all(detected, 'chan', split_axis=0, concat_axis=0, tiled=True)]
    reshape x8 -> x0, local copies, waits for them, and re-layouts: 3.31 us -> none  [body(): power.reshape(count, beams, 2, block).transpose(3, 1, 2, 0)]
    unnamed x17 -> x27, local copies, waits for them, and re-layouts: 2.43 us -> 5.1 us
    pallas_call x1 -> x2, Pallas kernels: 12.9 us -> 15.5 us  [detect(): pl.pallas_call(lambda *refs: detect_kernel(*refs, total=total), grid=(loc...]
    ppermute x4, waiting for transfers between devices: 17.8 us -> 15.1 us  [body(): backs.append(lax.ppermute(away, 'grp', [(g, g ^ 2) for g in range(groups)]))]
    add x8 -> x0, other arithmetic: 1.9 us -> none  [the longest x4 1.76 us: body(): whole = fold(both[:, :, :block]) + back.astype(jnp.float32)]
  transfers between devices with their start and end apart: 9 -> 10, of which waited for: 4 -> 4; matrix products, arithmetic and copies ran while one was open for 7% -> 3% of each run, Pallas kernels for 23% -> 36%
where the time goes in v2:
time: 139 us; the launch traced here: 138 us
  Pallas kernels  83.7 us (60%)
  waiting for transfers between devices  23 us (17%)
  starting transfers between devices  22.3 us (16%)
  local copies, waits for them, and re-layouts  6.5 us (5%)
  other arithmetic  2.59 us (2%)
    pallas_call x4, Pallas kernels, dedisperse(): pl.pallas_call(dedisperse_kernel, grid=(2 * units,), in_specs=[pl.BlockSp...  23.2 us
    pallas_call x1, Pallas kernels, dedispersion_factors(): pl.pallas_call(lambda *refs: factors_kernel(*refs, length=length, scale=s...  19.2 us
    all_to_all x2, starting transfers between devices, body(): lax.all_to_all(detected, 'chan', split_axis=0, concat_axis=0, tiled=True)  17.3 us
    pallas_call x2, Pallas kernels, detect(): pl.pallas_call(lambda *refs: detect_kernel(*refs, total=total), grid=(loc...  15.5 us
    ppermute x4, waiting for transfers between devices, body(): backs.append(lax.ppermute(away, 'grp', [(g, g ^ 2) for g in range(groups)]))  15.1 us
    pallas_call x4, Pallas kernels, join(): pl.pallas_call(join_kernel, out_shape=[jax.ShapeDtypeStruct((count // 2,...  9.25 us
    all_to_all x2, waiting for transfers between devices, body(): lax.all_to_all(detected, 'chan', split_axis=0, concat_axis=0, tiled=True)  7.87 us
    pallas_call x1, Pallas kernels, spectra(): pl.pallas_call(spectra_end_kernel, out_shape=jax.ShapeDtypeStruct((length...  7.8 us
  transfers between devices with their start and end apart: 10, of which 4 were waited for; matrix products, arithmetic and copies ran while one was open for 3% of the time, Pallas kernels for 36%

profile of v2, /device:TPU:1, one launch (start us, length us, event | category | flops | bytes accessed | tf_op | source)
XLA Modules:
  0.0 138.3 jit_solution(5493503113164675852)
XLA Ops:
  0.0 7.8 %detect0.1 = bf16[32,4,16,256]{3,2,1,0:T(8,128)(2,1)} custom-call(s32[1]{0:T(128)} %bitcast.5.refs_0_, s32[64,512]{1,0:T(8,128)} %refs_1_.3, bf16[4,4096,128]{2,1,0:T(8,128)(2,1)} %refs_2_.3), custom_call_target="tpu_custom_call" | custom-call | tf_op jit(solution)/shard_map/detect0/pallas_call | solution.py:78
  7.8 11.3 %all-to-all-start.1 = ((bf16[32,4,16,256]{3,2,1,0:T(8,128)(2,1)}), bf16[32,4,16,256]{3,2,1,0:T(8,128)(2,1)S(1)}, u32[]{:S(2)}, u32[]{:S(2)}) async-start(bf16[32,4,16,256]{3,2,1,0:T(8,128)(2,1)} %detect0.1), calls=%async_computation.1 | async-start | bytes 2097152 | tf_op jit(solution)/shard_map/all_to_all | solution.py:344
  19.1 7.8 %detect1.1 = bf16[32,4,16,256]{3,2,1,0:T(8,128)(2,1)} custom-call(s32[1]{0:T(128)} %bitcast.5.refs_0_, s32[64,512]{1,0:T(8,128)} %refs_1_.3, bf16[4,4096,128]{2,1,0:T(8,128)(2,1)} %refs_2_.3), custom_call_target="tpu_custom_call" | custom-call | tf_op jit(solution)/shard_map/detect1/pallas_call | solution.py:78
  27.4 7.9 %all-to-all-done.1 = bf16[32,4,16,256]{3,2,1,0:T(8,128)(2,1)S(1)} async-done(((bf16[32,4,16,256]{3,2,1,0:T(8,128)(2,1)}), bf16[32,4,16,256]{3,2,1,0:T(8,128)(2,1)S(1)}, u32[]{:S(2)}, u32[]{:S(2)}) %all-to-all-start.1) | async-done | bytes 1048608 | tf_op jit(solution)/shard_map/all_to_all | solution.py:344
  35.3 6.0 %all-to-all-start = ((bf16[32,4,16,256]{3,2,1,0:T(8,128)(2,1)}), bf16[32,4,16,256]{3,2,1,0:T(8,128)(2,1)S(1)}, u32[]{:S(2)}, u32[]{:S(2)}) async-start(bf16[32,4,16,256]{3,2,1,0:T(8,128)(2,1)} %detect1.1), calls=%async_computation | async-start | bytes 2097152 | tf_op jit(solution)/shard_map/all_to_all | solution.py:344
  42.3 19.2 %factors.1 = bf16[256,256,256]{2,1,0:T(8,128)(2,1)} custom-call(s32[128,256]{1,0:T(8,128)} %add_bitcast_fusion.refs_0_), custom_call_target="tpu_custom_call" | custom-call | tf_op jit(solution)/shard_map/factors/pallas_call | solution.py:199
  61.5 1.8 %fusion.2 = bf16[512,512]{1,0:T(8,128)(2,1)S(1)} fusion(s32[512]{0:T(512)S(1)} %fusion.7, pred[512]{0:T(512)(128)(4,1)S(1)} %iota_compare_fusion), kind=kLoop, calls=%fused_computation.4 | loop fusion | flops 11272192 | bytes 526848 | tf_op jit(solution)/shard_map/convert_element_type | solution.py:326
  63.3 0.8 fusion.8
  64.2 4.7 %spectra_start.1.begun = f32[8192,128]{1,0:T(8,128)} custom-call(bf16[128,16,256]{2,1,0:T(8,128)(2,1)} %bitcast.13, bf16[512,256]{1,0:T(8,128)(2,1)} %get-tuple-element.45.table), custom_call_target="tpu_custom_call" | custom-call | tf_op jit(solution)/shard_map/spectra_start/pallas_call | solution.py:142
  68.9 1.0 copy-done.1
  69.9 7.8 %spectra_end.1.spec = bf16[256,32,128]{2,1,0:T(8,128)(2,1)} custom-call(bf16[128,16,256]{2,1,0:T(8,128)(2,1)} %bitcast.14, bf16[512,256]{1,0:T(8,128)(2,1)} %get-tuple-element.46.table, f32[8192,128]{1,0:T(8,128)} %spectra_start.1.begun), custom_call_target="tpu_custom_call" | custom-call | tf_op jit(solution)/shard_map/spectra_end/pallas_call | solution.py:149
  77.7 5.8 %dedisperse0.1 = (bf16[64,32,128]{2,1,0:T(8,128)(2,1)}, bf16[64,32,128]{2,1,0:T(8,128)(2,1)}) custom-call(bf16[256,256,256]{2,1,0:T(8,128)(2,1)} %factors.1, bf16[256,32,128]{2,1,0:T(8,128)(2,1)} %spectra_end.1.spec), custom_call_target="tpu_custom_call" | custom-call | tf_op jit(solution)/shard_map/dedisperse0/pallas_call | solution.py:241
  83.5 1.2 collective-permute-start
  84.7 5.8 %dedisperse2.1 = (bf16[64,32,128]{2,1,0:T(8,128)(2,1)}, bf16[64,32,128]{2,1,0:T(8,128)(2,1)}) custom-call(bf16[256,256,256]{2,1,0:T(8,128)(2,1)} %factors.1, bf16[256,32,128]{2,1,0:T(8,128)(2,1)} %spectra_end.1.spec), custom_call_target="tpu_custom_call" | custom-call | tf_op jit(solution)/shard_map/dedisperse2/pallas_call | solution.py:241
  91.3 2.3 %join0.1 = (f32[32,32,128]{2,1,0:T(8,128)}, bf16[32,32,128]{2,1,0:T(8,128)(2,1)}) custom-call(bf16[64,32,128]{2,1,0:T(8,128)(2,1)} %get-tuple-element.25.keep, bf16[64,32,128]{2,1,0:T(8,128)(2,1)} %copy-done.6), custom_call_target="tpu_custom_call" | custom-call | tf_op jit(solution)/shard_map/join0/pallas_call | solution.py:268
  94.4 2.3 %join2.1 = (f32[32,32,128]{2,1,0:T(8,128)}, bf16[32,32,128]{2,1,0:T(8,128)(2,1)}) custom-call(bf16[64,32,128]{2,1,0:T(8,128)(2,1)} %get-tuple-element.28.keep, bf16[64,32,128]{2,1,0:T(8,128)(2,1)} %copy-done.5), custom_call_target="tpu_custom_call" | custom-call | tf_op jit(solution)/shard_map/join2/pallas_call | solution.py:268
  96.7 5.8 %dedisperse6.1 = (bf16[64,32,128]{2,1,0:T(8,128)(2,1)}, bf16[64,32,128]{2,1,0:T(8,128)(2,1)}) custom-call(bf16[256,256,256]{2,1,0:T(8,128)(2,1)} %factors.1, bf16[256,32,128]{2,1,0:T(8,128)(2,1)} %spectra_end.1.spec), custom_call_target="tpu_custom_call" | custom-call | tf_op jit(solution)/shard_map/dedisperse6/pallas_call | solution.py:241
  103.3 5.8 %dedisperse4.1 = (bf16[64,32,128]{2,1,0:T(8,128)(2,1)}, bf16[64,32,128]{2,1,0:T(8,128)(2,1)}) custom-call(bf16[256,256,256]{2,1,0:T(8,128)(2,1)} %factors.1, bf16[256,32,128]{2,1,0:T(8,128)(2,1)} %spectra_end.1.spec), custom_call_target="tpu_custom_call" | custom-call | tf_op jit(solution)/shard_map/dedisperse4/pallas_call | solution.py:241
  111.5 2.3 %join6.1 = (f32[32,32,128]{2,1,0:T(8,128)}, bf16[32,32,128]{2,1,0:T(8,128)(2,1)}) custom-call(bf16[64,32,128]{2,1,0:T(8,128)(2,1)} %get-tuple-element.38.keep, bf16[64,32,128]{2,1,0:T(8,128)(2,1)} %copy-done.4), custom_call_target="tpu_custom_call" | custom-call | tf_op jit(solution)/shard_map/join6/pallas_call | solution.py:268
  115.3 2.3 %join4.1 = (f32[32,32,128]{2,1,0:T(8,128)}, bf16[32,32,128]{2,1,0:T(8,128)(2,1)}) custom-call(bf16[64,32,128]{2,1,0:T(8,128)(2,1)} %get-tuple-element.33.keep, bf16[64,32,128]{2,1,0:T(8,128)(2,1)} %copy-done.3), custom_call_target="tpu_custom_call" | custom-call | tf_op jit(solution)/shard_map/join4/pallas_call | solution.py:268
  118.4 3.9 %collective-permute-done.4.refs_4_ = bf16[32,32,128]{2,1,0:T(8,128)(2,1)S(1)} collective-permute-done((bf16[32,32,128]{2,1,0:T(8,128)(2,1)S(1)}, bf16[32,32,128]{2,1,0:T(8,128)(2,1)S(1)}, u32[]{:S(2)}, u32[]{:S(2)}) %collective-permute-start.4) | collective-permute-done | bytes 262176 | tf_op jit(solution)/shard_map/ppermute | solution.py:374
  122.3 5.6 %collective-permute-done.7.refs_7_ = bf16[32,32,128]{2,1,0:T(8,128)(2,1)S(1)} collective-permute-done((bf16[32,32,128]{2,1,0:T(8,128)(2,1)}, bf16[32,32,128]{2,1,0:T(8,128)(2,1)S(1)}, u32[]{:S(2)}, u32[]{:S(2)}) %collective-permute-start.7) | collective-permute-done | bytes 262176 | tf_op jit(solution)/shard_map/ppermute | solution.py:374
  127.9 5.6 %collective-permute-done.6.refs_6_ = bf16[32,32,128]{2,1,0:T(8,128)(2,1)S(1)} collective-permute-done((bf16[32,32,128]{2,1,0:T(8,128)(2,1)}, bf16[32,32,128]{2,1,0:T(8,128)(2,1)S(1)}, u32[]{:S(2)}, u32[]{:S(2)}) %collective-permute-start.6) | collective-permute-done | bytes 262176 | tf_op jit(solution)/shard_map/ppermute | solution.py:374
  134.2 4.1 %power.1 = f32[64,16,256]{2,1,0:T(8,128)} custom-call(f32[32,32,128]{2,1,0:T(8,128)} %get-tuple-element.27.refs_0_, f32[32,32,128]{2,1,0:T(8,128)} %get-tuple-element.30.refs_1_, f32[32,32,128]{2,1,0:T(8,128)} %get-tuple-element.35.refs_2_, f32[32,32,128]{2,1,0:T(8,128)} %get-tuple-element.40.refs_3_, bf16[32,32,128]{2,1,0:T(8,128)(2,1)} %copy-done.8, ...), custom_call_target="tpu_custom_call" | custom-call | tf_op jit(solution)/shard_map/power/pallas_call | solution.py:309
  (46 shorter events, 9.3 us)
Async XLA Ops:
  7.8 19.1 %copy-start.2 = (s32[256,512]{1,0:T(8,128)S(1)}, s32[256,512]{1,0:T(8,128)}, u32[]{:S(2)}) copy-start(s32[256,512]{1,0:T(8,128)} %param.5) | copy-start | bytes 1572868
  7.8 27.5 %all-to-all-start.1 = ((bf16[32,4,16,256]{3,2,1,0:T(8,128)(2,1)}), bf16[32,4,16,256]{3,2,1,0:T(8,128)(2,1)S(1)}, u32[]{:S(2)}, u32[]{:S(2)}) async-start(bf16[32,4,16,256]{3,2,1,0:T(8,128)(2,1)} %detect0.1), calls=%async_computation.1 | async-start | bytes 2097152 | tf_op jit(solution)/shard_map/all_to_all | solution.py:344
  35.3 26.2 %copy-start = (bf16[32,4,16,256]{3,2,1,0:T(8,128)(2,1)}, bf16[32,4,16,256]{3,2,1,0:T(8,128)(2,1)S(1)}, u32[]{:S(2)}) copy-start(bf16[32,4,16,256]{3,2,1,0:T(8,128)(2,1)S(1)} %all-to-all-done.1) | copy-start | bytes 3145732
  35.3 33.6 %all-to-all-start = ((bf16[32,4,16,256]{3,2,1,0:T(8,128)(2,1)}), bf16[32,4,16,256]{3,2,1,0:T(8,128)(2,1)S(1)}, u32[]{:S(2)}, u32[]{:S(2)}) async-start(bf16[32,4,16,256]{3,2,1,0:T(8,128)(2,1)} %detect1.1), calls=%async_computation | async-start | bytes 2097152 | tf_op jit(solution)/shard_map/all_to_all | solution.py:344
  68.9 1.0 copy-start.1
  83.5 7.0 %collective-permute-start = (bf16[64,32,128]{2,1,0:T(8,128)(2,1)}, bf16[64,32,128]{2,1,0:T(8,128)(2,1)S(1)}, u32[]{:S(2)}, u32[]{:S(2)}) collective-permute-start(bf16[64,32,128]{2,1,0:T(8,128)(2,1)} %get-tuple-element.26), channel_id=1, source_target_pairs={{0,1},{1,0},{2,3},{3,2},{4,5},{5,4},{6,7},{7,6},{8,9},{9,8},{10,11... | collective-permute-start | bytes 1572872 | tf_op jit(solution)/shard_map/ppermute | solution.py:368
  90.5 3.1 %collective-permute-start.1 = (bf16[64,32,128]{2,1,0:T(8,128)(2,1)}, bf16[64,32,128]{2,1,0:T(8,128)(2,1)S(1)}, u32[]{:S(2)}, u32[]{:S(2)}) collective-permute-start(bf16[64,32,128]{2,1,0:T(8,128)(2,1)} %get-tuple-element.29), channel_id=1, source_target_pairs={{0,1},{1,0},{2,3},{3,2},{4,5},{5,4},{6,7},{7,6},{8,9},{9,8},{10,11... | collective-permute-start | bytes 1572872 | tf_op jit(solution)/shard_map/ppermute | solution.py:368
  90.5 0.8 copy-start.6
  93.6 0.8 copy-start.5
  102.6 6.6 %copy-start.12 = (bf16[32,32,128]{2,1,0:T(8,128)(2,1)S(1)}, bf16[32,32,128]{2,1,0:T(8,128)(2,1)}, u32[]{:S(2)}) copy-start(bf16[32,32,128]{2,1,0:T(8,128)(2,1)} %get-tuple-element.42) | copy-start | bytes 786436
  102.6 7.4 %copy-start.11 = (bf16[32,32,128]{2,1,0:T(8,128)(2,1)S(1)}, bf16[32,32,128]{2,1,0:T(8,128)(2,1)}, u32[]{:S(2)}) copy-start(bf16[32,32,128]{2,1,0:T(8,128)(2,1)} %get-tuple-element.41) | copy-start | bytes 786436
  102.6 8.1 %collective-permute-start.3 = (bf16[64,32,128]{2,1,0:T(8,128)(2,1)}, bf16[64,32,128]{2,1,0:T(8,128)(2,1)S(1)}, u32[]{:S(2)}, u32[]{:S(2)}) collective-permute-start(bf16[64,32,128]{2,1,0:T(8,128)(2,1)} %get-tuple-element.39), channel_id=1, source_target_pairs={{0,1},{1,0},{2,3},{3,2},{4,5},{5,4},{6,7},{7,6},{8,9},{9,8},{10,11... | collective-permute-start | bytes 1572872 | tf_op jit(solution)/shard_map/ppermute | solution.py:368
  109.1 5.4 %collective-permute-start.2 = (bf16[64,32,128]{2,1,0:T(8,128)(2,1)}, bf16[64,32,128]{2,1,0:T(8,128)(2,1)S(1)}, u32[]{:S(2)}, u32[]{:S(2)}) collective-permute-start(bf16[64,32,128]{2,1,0:T(8,128)(2,1)} %get-tuple-element.34), channel_id=1, source_target_pairs={{0,1},{1,0},{2,3},{3,2},{4,5},{5,4},{6,7},{7,6},{8,9},{9,8},{10,11... | collective-permute-start | bytes 1572872 | tf_op jit(solution)/shard_map/ppermute | solution.py:368
  109.2 9.2 %collective-permute-start.5 = (bf16[32,32,128]{2,1,0:T(8,128)(2,1)S(1)}, bf16[32,32,128]{2,1,0:T(8,128)(2,1)S(1)}, u32[]{:S(2)}, u32[]{:S(2)}) collective-permute-start(bf16[32,32,128]{2,1,0:T(8,128)(2,1)S(1)} %copy-done.12), channel_id=1, source_target_pairs={{0,2},{1,3},{2,0},{3,1},{4,6},{5,7},{6,4},{7,5},{8,10},{9,11},{10,... | collective-permute-start | bytes 786440 | tf_op jit(solution)/shard_map/ppermute | solution.py:374
  109.9 12.3 %collective-permute-start.4 = (bf16[32,32,128]{2,1,0:T(8,128)(2,1)S(1)}, bf16[32,32,128]{2,1,0:T(8,128)(2,1)S(1)}, u32[]{:S(2)}, u32[]{:S(2)}) collective-permute-start(bf16[32,32,128]{2,1,0:T(8,128)(2,1)S(1)} %copy-done.11), channel_id=1, source_target_pairs={{0,2},{1,3},{2,0},{3,1},{4,6},{5,7},{6,4},{7,5},{8,10},{9,11},{10,... | collective-permute-start | bytes 786440 | tf_op jit(solution)/shard_map/ppermute | solution.py:374
  110.7 0.8 copy-start.4
  113.8 14.1 %collective-permute-start.7 = (bf16[32,32,128]{2,1,0:T(8,128)(2,1)}, bf16[32,32,128]{2,1,0:T(8,128)(2,1)S(1)}, u32[]{:S(2)}, u32[]{:S(2)}) collective-permute-start(bf16[32,32,128]{2,1,0:T(8,128)(2,1)} %get-tuple-element.44), channel_id=1, source_target_pairs={{0,2},{1,3},{2,0},{3,1},{4,6},{5,7},{6,4},{7,5},{8,10},{9,11},{10,... | collective-permute-start | bytes 786440 | tf_op jit(solution)/shard_map/ppermute | solution.py:374
  114.5 0.8 copy-start.3
  117.6 15.9 %collective-permute-start.6 = (bf16[32,32,128]{2,1,0:T(8,128)(2,1)}, bf16[32,32,128]{2,1,0:T(8,128)(2,1)S(1)}, u32[]{:S(2)}, u32[]{:S(2)}) collective-permute-start(bf16[32,32,128]{2,1,0:T(8,128)(2,1)} %get-tuple-element.43), channel_id=1, source_target_pairs={{0,2},{1,3},{2,0},{3,1},{4,6},{5,7},{6,4},{7,5},{8,10},{9,11},{10,... | collective-permute-start | bytes 786440 | tf_op jit(solution)/shard_map/ppermute | solution.py:374
  118.4 15.2 %copy-start.7 = (bf16[32,32,128]{2,1,0:T(8,128)(2,1)}, bf16[32,32,128]{2,1,0:T(8,128)(2,1)S(1)}, u32[]{:S(2)}) copy-start(bf16[32,32,128]{2,1,0:T(8,128)(2,1)S(1)} %collective-permute-done.5.refs_5_) | copy-start | bytes 786436
  122.3 11.2 %copy-start.8 = (bf16[32,32,128]{2,1,0:T(8,128)(2,1)}, bf16[32,32,128]{2,1,0:T(8,128)(2,1)S(1)}, u32[]{:S(2)}) copy-start(bf16[32,32,128]{2,1,0:T(8,128)(2,1)S(1)} %collective-permute-done.4.refs_4_) | copy-start | bytes 786436
  127.9 5.6 %copy-start.9 = (bf16[32,32,128]{2,1,0:T(8,128)(2,1)}, bf16[32,32,128]{2,1,0:T(8,128)(2,1)S(1)}, u32[]{:S(2)}) copy-start(bf16[32,32,128]{2,1,0:T(8,128)(2,1)S(1)} %collective-permute-done.7.refs_7_) | copy-start | bytes 786436
  133.5 0.7 copy-start.10

commit v3 on v1

v3 whole, which is shorter than its diff:
```python
import math

import jax
import jax.numpy as jnp
import numpy as np
from jax import lax
from jax.experimental import pallas as pl
from jax.experimental.pallas import tpu as pltpu
from jax.sharding import PartitionSpec as P

INTEG = 8
PHASES = 4096
BLOCKS = 8
VMEM_LIMIT = 56 * 1024 * 1024
PARAMS = pltpu.CompilerParams(vmem_limit_bytes=VMEM_LIMIT)


def sin_cos(steps, turn):
    quarter = turn // 4
    steps = steps & (turn - 1)
    quadrant = (steps + quarter // 2) >> (quarter.bit_length() - 1)
    x = (steps - quadrant * quarter).astype(jnp.float32) * jnp.float32(2.0 * math.pi / turn)
    y = x * x
    s = x * (1.0 + y * (-1.0 / 6 + y * (1.0 / 120 + y * (-1.0 / 5040 + y * (1.0 / 362880)))))
    c = 1.0 + y * (-0.5 + y * (1.0 / 24 + y * (-1.0 / 720 + y * (1.0 / 40320))))
    swap = (quadrant & 1) == 1
    sine = jnp.where(swap, c, s)
    cosine = jnp.where(swap, s, c)
    sine = jnp.where((quadrant & 2) == 2, -sine, sine)
    cosine = jnp.where(((quadrant + 1) & 2) == 2, -cosine, cosine)
    return sine, cosine


def spectra_kernel(first, delays, table, volts, out, spread, rows, weights, series, mixed, *, total):
    dishes, beams = delays.shape
    channel = pl.program_id(0)
    sine, cosine = sin_cos(delays[...] * (first[0] + channel + total), PHASES)
    scale = jnp.float32(1.0 / math.sqrt(dishes))
    real = (cosine * scale).astype(jnp.bfloat16)
    imag = (-(sine * scale)).astype(jnp.bfloat16)
    width = min(beams, 128)
    tiles = beams // width
    for n in range(tiles):
        cols = slice(n * width, (n + 1) * width)
        weights[n, :dishes, :width] = real[:, cols]
        weights[n, :dishes, width:] = imag[:, cols]
        weights[n, dishes:, :width] = -imag[:, cols]
        weights[n, dishes:, width:] = real[:, cols]
    spread[...] = volts[0].astype(jnp.float32)
    blocks, span, _ = rows.shape
    piece = span // INTEG
    for tb in range(blocks):
        for s in range(INTEG):
            rows[tb, s * piece : (s + 1) * piece, :] = spread[
                pl.ds(tb * span + s, piece, stride=INTEG), :
            ].astype(jnp.bfloat16)
    for n in range(tiles):
        for tb in range(blocks):
            beam = jnp.dot(rows[tb], weights[n], preferred_element_type=jnp.float32)
            power = beam[:, :width] * beam[:, :width] + beam[:, width:] * beam[:, width:]
            mean = jnp.sum(power.reshape(INTEG, piece, width), axis=0) * jnp.float32(1.0 / INTEG)
            series[tb * piece : (tb + 1) * piece, n * width : (n + 1) * width] = mean.astype(
                jnp.bfloat16
            )
    result = jnp.dot(table[...], series[...], preferred_element_type=jnp.float32)
    owners, share, _ = out.shape
    kinds = result.shape[0] // owners
    for kind in range(kinds):
        for n in range(tiles):
            mixed[n, pl.ds(channel * kinds + kind, owners, stride=share), :] = result[
                kind * owners : (kind + 1) * owners, n * width : (n + 1) * width
            ]

    @pl.when(channel == pl.num_programs(0) - 1)
    def _():
        for n in range(tiles):
            out[:, :, n * width : (n + 1) * width] = (
                mixed[n].reshape(owners, share, width).astype(jnp.bfloat16)
            )


def spectra(voltages, delays, table, first, total, devices):
    local, time, doubled = voltages.shape
    dishes, beams = delays.shape
    steps = time // INTEG
    width = min(beams, 128)
    share = local * steps // devices
    return pl.pallas_call(
        lambda *refs: spectra_kernel(*refs, total=total),
        grid=(local,),
        in_specs=[
            pl.BlockSpec(memory_space=pltpu.SMEM),
            pl.BlockSpec((dishes, beams), lambda i: (0, 0)),
            pl.BlockSpec((steps, steps), lambda i: (0, 0)),
            pl.BlockSpec((1, time, doubled), lambda i: (i, 0, 0)),
        ],
        out_specs=pl.BlockSpec((devices, share, beams), lambda i: (0, 0, 0)),
        out_shape=jax.ShapeDtypeStruct((devices, share, beams), jnp.bfloat16),
        scratch_shapes=[
            pltpu.VMEM((time, doubled), jnp.float32),
            pltpu.VMEM((BLOCKS, time // BLOCKS, doubled), jnp.bfloat16),
            pltpu.VMEM((beams // width, doubled, 2 * width), jnp.bfloat16),
            pltpu.VMEM((steps, beams), jnp.bfloat16),
            pltpu.VMEM((beams // width, devices * share, width), jnp.float32),
        ],
        compiler_params=PARAMS,
        name="spectra",
    )(first.reshape(1), delays, table, voltages)


def factors_kernel(device, shifts, out, *, devices, length, scale):
    trials, channels = shifts.shape
    number = pl.program_id(0) * devices + device[0] + 1
    sine, cosine = sin_cos(shifts[...] * number, length)
    sine = (sine * scale).astype(jnp.bfloat16)
    cosine = (cosine * scale).astype(jnp.bfloat16)
    out[0, :trials, :channels] = cosine
    out[0, :trials, channels:] = -sine
    out[0, trials:, :channels] = sine
    out[0, trials:, channels:] = cosine


def dedispersion_factors(shifts, device, devices, length, scale):
    trials, channels = shifts.shape
    held = length // 2 // devices
    return pl.pallas_call(
        lambda *refs: factors_kernel(*refs, devices=devices, length=length, scale=scale),
        grid=(held,),
        in_specs=[
            pl.BlockSpec(memory_space=pltpu.SMEM),
            pl.BlockSpec((trials, channels), lambda i: (0, 0)),
        ],
        out_specs=pl.BlockSpec((1, 2 * trials, 2 * channels), lambda i: (i, 0, 0)),
        out_shape=jax.ShapeDtypeStruct((held, 2 * trials, 2 * channels), jnp.bfloat16),
        compiler_params=PARAMS,
        name="factors",
    )(device.reshape(1), shifts)


def powers_kernel(factors, spec, out, wide, right, powers):
    bins, doubled, _ = factors.shape
    trials = doubled // 2
    devices, share, beams = spec.shape
    tiles, _, width = wide.shape
    channels = right.shape[0] // 2
    kinds = 2 * bins
    for n in range(tiles):
        piece = spec[:, :, n * width : (n + 1) * width]
        wide[n] = piece.reshape(devices * share, width).astype(jnp.float32)
    for h in range(bins):
        for n in range(tiles):
            for part in range(2):
                right[part * channels : (part + 1) * channels, n * width : (n + 1) * width] = wide[
                    n, pl.ds(part * bins + h, channels, stride=kinds), :
                ].astype(jnp.bfloat16)
        result = jnp.dot(factors[h], right[...], preferred_element_type=jnp.float32)
        real = result[:trials]
        imag = result[trials:]
        powers[h] = real * real + imag * imag
    owners, groups, held, lanes = out.shape
    block = trials // groups
    for g in range(groups):
        stack = jnp.concatenate(
            [powers[h, g * block : (g + 1) * block, :] for h in range(bins)], axis=0
        )
        out[:, g] = stack.T.astype(jnp.bfloat16).reshape(owners, held, lanes)


def bin_powers(factors, spec, owners, groups):
    bins, doubled, columns = factors.shape
    devices, share, beams = spec.shape
    width = min(beams, 128)
    trials = doubled // 2
    return pl.pallas_call(
        powers_kernel,
        out_shape=jax.ShapeDtypeStruct(
            (owners, groups, beams // owners, bins * trials // groups), jnp.bfloat16
        ),
        scratch_shapes=[
            pltpu.VMEM((beams // width, devices * share, width), jnp.float32),
            pltpu.VMEM((columns, beams), jnp.bfloat16),
            pltpu.VMEM((bins, trials, beams), jnp.float32),
        ],
        compiler_params=PARAMS,
        name="powers",
    )(factors, spec)


def arrange_kernel(moved, out, wide, turned):
    devices, beams, lanes = moved.shape
    block = out.shape[0]
    tiles, _, width = wide.shape
    each = width // block
    for n in range(tiles):
        piece = moved[:, :, n * width : (n + 1) * width]
        wide[n] = piece.reshape(devices * beams, width).astype(jnp.float32)
    for n in range(tiles):
        for b in range(beams):
            flipped = wide[n, pl.ds(b, devices, stride=beams), :].T
            for e in range(each):
                turned[n * each + e, b * block : (b + 1) * block, :] = flipped[
                    e * block : (e + 1) * block
                ]
    for m in range(block):
        for h in range(tiles * each):
            out[m, :, h * devices : (h + 1) * devices] = turned[
                h, pl.ds(m, beams, stride=block), :
            ]


def arrange(moved, block):
    devices, beams, lanes = moved.shape
    width = 128
    bins = lanes // block
    return pl.pallas_call(
        arrange_kernel,
        out_shape=jax.ShapeDtypeStruct((block, beams, bins * devices), jnp.float32),
        scratch_shapes=[
            pltpu.VMEM((lanes // width, devices * beams, width), jnp.float32),
            pltpu.VMEM((bins, beams * block, devices), jnp.float32),
        ],
        compiler_params=PARAMS,
        name="arrange",
    )(moved)


def dft_table(length):
    sample = np.arange(length)
    angle = (sample * np.arange(1, length // 2 + 1)[:, None]) % length * (2.0 * np.pi / length)
    rows = np.concatenate([np.cos(angle), -np.sin(angle)], axis=0) / math.sqrt(length)
    return jnp.asarray(rows.astype(np.float32)).astype(jnp.bfloat16)


def body(voltages, delays, shifts, table):
    owners = lax.axis_size("chan")
    groups = lax.axis_size("grp")
    devices = owners * groups
    device = lax.axis_index("chan") * groups + lax.axis_index("grp")
    local, time, _ = voltages.shape
    total = local * devices
    length = time // INTEG
    both = ("chan", "grp")

    factors = dedispersion_factors(shifts, device, devices, length, 1.0 / math.sqrt(total))
    sent = spectra(voltages, delays, table, device * local, total, devices)
    spec = lax.all_to_all(sent, both, split_axis=0, concat_axis=0, tiled=True)
    powers = bin_powers(factors, spec, owners, groups)
    powers = powers.reshape((devices,) + powers.shape[2:])
    moved = lax.all_to_all(powers, both, split_axis=0, concat_axis=0, tiled=True)
    return arrange(moved, shifts.shape[0] // groups)


def solution(mesh):
    placed = (P(("chan", "grp"), None, None), P(), P(), P())
    run = jax.shard_map(
        body, mesh=mesh, in_specs=placed, out_specs=P("grp", "chan", None), check_vma=False
    )

    def whole(voltages, delays, shifts):
        return run(voltages, delays, shifts, dft_table(voltages.shape[1] // INTEG))

    return whole
```

time: 142 us -> 86.8 us (0.61)
  Pallas kernels: 64.3 us -> 27.9 us
  blocking collectives: 0 us -> 19.8 us
  waiting for transfers between devices: 42 us -> 25.9 us
  local copies, waits for them, and re-layouts: 9.19 us -> 1.31 us
  other arithmetic: 7.76 us -> 0 us
  starting transfers between devices: 17.6 us -> 11.5 us
    pallas_call x6 -> x4, Pallas kernels: 64.3 us -> 27.9 us  [the longest x1 16.1 us: spectra(): pl.pallas_call(lambda *refs: spectra_kernel(*refs, total=total), grid=(lo...]
    all_to_all x0 -> x1, blocking collectives: none -> 19.8 us  [body(): lax.all_to_all(powers, both, split_axis=0, concat_axis=0, tiled=True)]
    ppermute x8 -> x0, waiting for transfers between devices: 17.8 us -> none  [the longest x4 17.8 us: body(): back = lax.ppermute(away, 'grp', [(g, g ^ 2) for g in range(groups)])]
    ppermute x8 -> x0, starting transfers between devices: 6.25 us -> none  [the longest x4 3.43 us: body(): back = lax.ppermute(away, 'grp', [(g, g ^ 2) for g in range(groups)])]
    reshape x10 -> x0, local copies, waits for them, and re-layouts: 3.62 us -> none  [the longest x8 3.31 us: body(): power.reshape(count, beams, 2, block).transpose(3, 1, 2, 0)]
    convert_element_type x1 -> x0, other arithmetic: 2.45 us -> none  [dft_table(): (jnp.where(row < bins, cosine, -sine) * jnp.float32(1.0 / math.sqrt(lengt...]
    add x9 -> x0, other arithmetic: 1.91 us -> none  [the longest x4 1.76 us: body(): whole = fold(both[:, :, :block]) + back.astype(jnp.float32)]
    concatenate x5 -> x0, other arithmetic: 1.84 us -> none  [the longest x1 1.25 us: body(): return jnp.concatenate(powers, axis=2)]
  transfers between devices with their start and end apart: 9 -> 1, of which waited for: 4 -> 1; matrix products, arithmetic and copies ran while one was open for 7% -> 0% of each run, Pallas kernels for 23% -> 4%
where the time goes in v3:
time: 86.8 us; the launch traced here: 86.5 us
  Pallas kernels  27.9 us (32%)
  waiting for transfers between devices  25.9 us (30%)
  blocking collectives  19.8 us (23%)
  starting transfers between devices  11.5 us (13%)
  local copies, waits for them, and re-layouts  1.31 us (2%)
    all_to_all x1, waiting for transfers between devices, body(): spec = lax.all_to_all(sent, both, split_axis=0, concat_axis=0, tiled=True)  25.9 us
    all_to_all x1, blocking collectives, body(): lax.all_to_all(powers, both, split_axis=0, concat_axis=0, tiled=True)  19.8 us
    pallas_call x1, Pallas kernels, spectra(): pl.pallas_call(lambda *refs: spectra_kernel(*refs, total=total), grid=(lo...  16.1 us
    all_to_all x1, starting transfers between devices, body(): spec = lax.all_to_all(sent, both, split_axis=0, concat_axis=0, tiled=True)  11.5 us
    pallas_call x1, Pallas kernels, bin_powers(): pl.pallas_call(powers_kernel, out_shape=jax.ShapeDtypeStruct((owners, gro...  4.9 us
    pallas_call x1, Pallas kernels, dedispersion_factors(): pl.pallas_call(lambda *refs: factors_kernel(*refs, devices=devices, lengt...  3.79 us
    pallas_call x1, Pallas kernels, arrange(): pl.pallas_call(arrange_kernel, out_shape=jax.ShapeDtypeStruct((block, bea...  3.13 us
  transfers between devices with their start and end apart: 1, of which 1 were waited for; matrix products, arithmetic and copies ran while one was open for 0% of the time, Pallas kernels for 4%

profile of v3, /device:TPU:1, one launch (start us, length us, event | category | flops | bytes accessed | tf_op | source)
XLA Modules:
  0.0 86.5 jit_solution(2193310241672022373)
XLA Ops:
  0.0 16.1 %spectra.1 = bf16[128,16,512]{2,1,0:T(8,128)(2,1)} custom-call(s32[1]{0:T(128)} %bitcast.1.refs_0_, s32[64,512]{1,0:T(8,128)} %refs_1_.3, bf16[512,512]{1,0:T(8,128)(2,1)} %constant.14.clone.refs_2_, bf16[4,4096,128]{2,1,0:T(8,128)(2,1)} %refs_3_.1), custom_call_target="tpu_custom_call" | custom-call | tf_op jit(solution)/shard_map/spectra/pallas_call | solution.py:88
  16.1 11.5 %all-to-all-start = ((bf16[128,16,512]{2,1,0:T(8,128)(2,1)}), bf16[128,16,512]{2,1,0:T(8,128)(2,1)S(1)}, u32[]{:S(2)}, u32[]{:S(2)}) async-start(bf16[128,16,512]{2,1,0:T(8,128)(2,1)} %spectra.1), calls=%async_computation | async-start | bytes 4194304 | tf_op jit(solution)/shard_map/all_to_all | solution.py:246
  27.6 3.8 %factors.1 = bf16[2,512,1024]{2,1,0:T(8,128)(2,1)} custom-call(s32[1]{0:T(128)} %bitcast.refs_0_, s32[256,512]{1,0:T(8,128)} %refs_1_.2), custom_call_target="tpu_custom_call" | custom-call | tf_op jit(solution)/shard_map/factors/pallas_call | solution.py:126
  31.4 25.9 %all-to-all-done.spec = bf16[128,16,512]{2,1,0:T(8,128)(2,1)S(1)} async-done(((bf16[128,16,512]{2,1,0:T(8,128)(2,1)}), bf16[128,16,512]{2,1,0:T(8,128)(2,1)S(1)}, u32[]{:S(2)}, u32[]{:S(2)}) %all-to-all-start) | async-done | bytes 2097184 | tf_op jit(solution)/shard_map/all_to_all | solution.py:246
  57.3 0.0 copy-start
  57.3 1.3 %copy-done = bf16[128,16,512]{2,1,0:T(8,128)(2,1)} copy-done((bf16[128,16,512]{2,1,0:T(8,128)(2,1)}, bf16[128,16,512]{2,1,0:T(8,128)(2,1)S(1)}, u32[]{:S(2)}) %copy-start) | copy-done | bytes 2097176
  58.6 4.9 %powers.1 = bf16[32,4,16,128]{3,2,1,0:T(8,128)(2,1)} custom-call(bf16[2,512,1024]{2,1,0:T(8,128)(2,1)} %factors.1, bf16[128,16,512]{2,1,0:T(8,128)(2,1)} %copy-done), custom_call_target="tpu_custom_call" | custom-call | tf_op jit(solution)/shard_map/powers/pallas_call | solution.py:174
  63.5 19.8 %all_to_all.10.moved = bf16[128,16,128]{2,1,0:T(8,128)(2,1)} all-to-all(bf16[128,16,128]{2,1,0:T(8,128)(2,1)} %bitcast.3), channel_id=1, replica_groups=mesh['chan'=32,'grp'=4] {'chan','grp'}, dimensions={0} | all-to-all | bytes 1048576 | tf_op jit(solution)/shard_map/all_to_all | solution.py:249
  83.4 3.1 %arrange.1 = f32[64,16,256]{2,1,0:T(8,128)} custom-call(bf16[128,16,128]{2,1,0:T(8,128)(2,1)} %all_to_all.10.moved), custom_call_target="tpu_custom_call" | custom-call | tf_op jit(solution)/shard_map/arrange/pallas_call | solution.py:215
Async XLA Ops:
  16.1 41.2 %all-to-all-start = ((bf16[128,16,512]{2,1,0:T(8,128)(2,1)}), bf16[128,16,512]{2,1,0:T(8,128)(2,1)S(1)}, u32[]{:S(2)}, u32[]{:S(2)}) async-start(bf16[128,16,512]{2,1,0:T(8,128)(2,1)} %spectra.1), calls=%async_computation | async-start | bytes 4194304 | tf_op jit(solution)/shard_map/all_to_all | solution.py:246
  57.3 1.3 %copy-start = (bf16[128,16,512]{2,1,0:T(8,128)(2,1)}, bf16[128,16,512]{2,1,0:T(8,128)(2,1)S(1)}, u32[]{:S(2)}) copy-start(bf16[128,16,512]{2,1,0:T(8,128)(2,1)S(1)} %all-to-all-done.spec) | copy-start | bytes 6291460

commit v4 on v3

--- a/solution.py
+++ b/solution.py
@@ -65,9 +65,12 @@
     result = jnp.dot(table[...], series[...], preferred_element_type=jnp.float32)
     owners, share, _ = out.shape
     kinds = result.shape[0] // owners
+    local = share // kinds
     for kind in range(kinds):
+        part, h = divmod(kind, kinds // 2)
+        row = (2 * h + part) * local + channel
         for n in range(tiles):
-            mixed[n, pl.ds(channel * kinds + kind, owners, stride=share), :] = result[
+            mixed[n, pl.ds(row, owners, stride=share), :] = result[
                 kind * owners : (kind + 1) * owners, n * width : (n + 1) * width
             ]
 
@@ -108,52 +111,63 @@
     )(first.reshape(1), delays, table, voltages)
 
 
-def factors_kernel(device, shifts, out, *, devices, length, scale):
-    trials, channels = shifts.shape
+def factors_kernel(device, shifts, out, *, devices, length, scale, local):
+    trials, columns = shifts.shape
     number = pl.program_id(0) * devices + device[0] + 1
     sine, cosine = sin_cos(shifts[...] * number, length)
-    sine = (sine * scale).astype(jnp.bfloat16)
-    cosine = (cosine * scale).astype(jnp.bfloat16)
-    out[0, :trials, :channels] = cosine
-    out[0, :trials, channels:] = -sine
-    out[0, trials:, :channels] = sine
-    out[0, trials:, channels:] = cosine
+    sine = sine * scale
+    cosine = cosine * scale
+    column = lax.broadcasted_iota(jnp.int32, (trials, columns), 1)
+    real = (column & local) == 0
+    out[0, :trials] = jnp.where(real, cosine, -sine).astype(jnp.bfloat16)
+    out[0, trials:] = jnp.where(real, sine, cosine).astype(jnp.bfloat16)
 
 
 def dedispersion_factors(shifts, device, devices, length, scale):
     trials, channels = shifts.shape
     held = length // 2 // devices
-    return pl.pallas_call(
-        lambda *refs: factors_kernel(*refs, devices=devices, length=length, scale=scale),
+    local = channels // devices
+    columns = 2 * channels
+    doubled = jnp.broadcast_to(
+        shifts.reshape(trials, devices, 1, local), (trials, devices, 2, local)
+    ).reshape(trials, columns)
+    return pl.pallas_call(
+        lambda *refs: factors_kernel(
+            *refs, devices=devices, length=length, scale=scale, local=local
+        ),
         grid=(held,),
         in_specs=[
             pl.BlockSpec(memory_space=pltpu.SMEM),
-            pl.BlockSpec((trials, channels), lambda i: (0, 0)),
-        ],
-        out_specs=pl.BlockSpec((1, 2 * trials, 2 * channels), lambda i: (i, 0, 0)),
-        out_shape=jax.ShapeDtypeStruct((held, 2 * trials, 2 * channels), jnp.bfloat16),
+            pl.BlockSpec((trials, columns), lambda i: (0, 0)),
+        ],
+        out_specs=pl.BlockSpec((1, 2 * trials, columns), lambda i: (i, 0, 0)),
+        out_shape=jax.ShapeDtypeStruct((held, 2 * trials, columns), jnp.bfloat16),
         compiler_params=PARAMS,
         name="factors",
-    )(device.reshape(1), shifts)
-
-
-def powers_kernel(factors, spec, out, wide, right, powers):
-    bins, doubled, _ = factors.shape
+    )(device.reshape(1), doubled)
+
+
+def powers_kernel(stored, spec, out, right, powers, factors, arrived):
+    bins, doubled, columns = factors.shape
     trials = doubled // 2
     devices, share, beams = spec.shape
-    tiles, _, width = wide.shape
-    channels = right.shape[0] // 2
-    kinds = 2 * bins
-    for n in range(tiles):
-        piece = spec[:, :, n * width : (n + 1) * width]
-        wide[n] = piece.reshape(devices * share, width).astype(jnp.float32)
+    width = min(beams, 128)
+    each = share // bins
+    fetches = [
+        pltpu.make_async_copy(stored.at[h], factors.at[h], arrived.at[h]) for h in range(bins)
+    ]
+    for fetch in fetches:
+        fetch.start()
+    for n in range(beams // width):
+        cols = slice(n * width, (n + 1) * width)
+        piece = spec[:, :, cols].astype(jnp.float32)
+        for h in range(bins):
+            right[h, :, cols] = (
+                piece[:, h * each : (h + 1) * each].reshape(columns, width).astype(jnp.bfloat16)
+            )
     for h in range(bins):
-        for n in range(tiles):
-            for part in range(2):
-                right[part * channels : (part + 1) * channels, n * width : (n + 1) * width] = wide[
-                    n, pl.ds(part * bins + h, channels, stride=kinds), :
-                ].astype(jnp.bfloat16)
-        result = jnp.dot(factors[h], right[...], preferred_element_type=jnp.float32)
+        fetches[h].wait()
+        result = jnp.dot(factors[h], right[h], preferred_element_type=jnp.float32)
         real = result[:trials]
         imag = result[trials:]
         powers[h] = real * real + imag * imag
@@ -168,18 +182,19 @@
 
 def bin_powers(factors, spec, owners, groups):
     bins, doubled, columns = factors.shape
-    devices, share, beams = spec.shape
-    width = min(beams, 128)
+    beams = spec.shape[2]
     trials = doubled // 2
     return pl.pallas_call(
         powers_kernel,
-        out_shape=jax.ShapeDtypeStruct(
+        in_specs=[pl.BlockSpec(memory_space=pl.ANY), pl.BlockSpec(memory_space=pltpu.VMEM)],
+        out_shape=pltpu.VMEM(
             (owners, groups, beams // owners, bins * trials // groups), jnp.bfloat16
         ),
         scratch_shapes=[
-            pltpu.VMEM((beams // width, devices * share, width), jnp.float32),
-            pltpu.VMEM((columns, beams), jnp.bfloat16),
+            pltpu.VMEM((bins, columns, beams), jnp.bfloat16),
             pltpu.VMEM((bins, trials, beams), jnp.float32),
+            pltpu.VMEM(factors.shape, jnp.bfloat16),
+            pltpu.SemaphoreType.DMA((bins,)),
         ],
         compiler_params=PARAMS,
         name="powers",
@@ -244,9 +259,11 @@
     factors = dedispersion_factors(shifts, device, devices, length, 1.0 / math.sqrt(total))
     sent = spectra(voltages, delays, table, device * local, total, devices)
     spec = lax.all_to_all(sent, both, split_axis=0, concat_axis=0, tiled=True)
+    spec = pltpu.with_memory_space_constraint(spec, pltpu.VMEM)
     powers = bin_powers(factors, spec, owners, groups)
     powers = powers.reshape((devices,) + powers.shape[2:])
     moved = lax.all_to_all(powers, both, split_axis=0, concat_axis=0, tiled=True)
+    moved = pltpu.with_memory_space_constraint(moved, pltpu.VMEM)
     return arrange(moved, shifts.shape[0] // groups)
 
 

time: 86.8 us -> 81.1 us (0.934)
  waiting for transfers between devices: 25.9 us -> 18 us
  local copies, waits for them, and re-layouts: 1.31 us -> 6.19 us
  Pallas kernels: 27.9 us -> 26.5 us
  blocking collectives: 19.8 us -> 18.6 us
    all_to_all x1, waiting for transfers between devices: 25.9 us -> 18 us  [body(): spec = lax.all_to_all(sent, both, split_axis=0, concat_axis=0, tiled=True)]
    reshape x0 -> x2, local copies, waits for them, and re-layouts: none -> 3.87 us  [dedispersion_factors(): doubled = jnp.broadcast_to(shifts.reshape(trials, devices, 1, local), (tr...]
    pallas_call x1, Pallas kernels: 4.9 us -> 2.78 us  [bin_powers(): pl.pallas_call(powers_kernel, in_specs=[pl.BlockSpec(memory_space=pl.ANY)...]
    broadcast_in_dim x0 -> x2, local copies, waits for them, and re-layouts: none -> 2.12 us  [dedispersion_factors(): jnp.broadcast_to(shifts.reshape(trials, devices, 1, local), (trials, devi...]
    pallas_call x1, Pallas kernels: 3.79 us -> 5.57 us  [dedispersion_factors(): pl.pallas_call(lambda *refs: factors_kernel(*refs, devices=devices, lengt...]
    all_to_all x1, blocking collectives: 19.8 us -> 18.6 us  [body(): lax.all_to_all(powers, both, split_axis=0, concat_axis=0, tiled=True)]
    unnamed x2 -> x3, local copies, waits for them, and re-layouts: 1.31 us -> 0.2 us
    pallas_call x1, Pallas kernels: 3.13 us -> 2.09 us  [arrange(): pl.pallas_call(arrange_kernel, out_shape=jax.ShapeDtypeStruct((block, bea...]
  transfers between devices with their start and end apart: 1 -> 1, of which waited for: 1 -> 1; matrix products, arithmetic and copies ran while one was open for 0% -> 8% of each run, Pallas kernels for 4% -> 7%
where the time goes in v4:
time: 81.1 us; the launch traced here: 80.8 us
  Pallas kernels  26.5 us (33%)
  blocking collectives  18.6 us (23%)
  waiting for transfers between devices  18 us (22%)
  starting transfers between devices  11.5 us (14%)
  local copies, waits for them, and re-layouts  6.19 us (8%)
    all_to_all x1, blocking collectives, body(): lax.all_to_all(powers, both, split_axis=0, concat_axis=0, tiled=True)  18.6 us
    all_to_all x1, waiting for transfers between devices, body(): spec = lax.all_to_all(sent, both, split_axis=0, concat_axis=0, tiled=True)  18 us
    pallas_call x1, Pallas kernels, spectra(): pl.pallas_call(lambda *refs: spectra_kernel(*refs, total=total), grid=(lo...  16.1 us
    all_to_all x1, starting transfers between devices, body(): spec = lax.all_to_all(sent, both, split_axis=0, concat_axis=0, tiled=True)  11.5 us
    pallas_call x1, Pallas kernels, dedispersion_factors(): pl.pallas_call(lambda *refs: factors_kernel(*refs, devices=devices, lengt...  5.57 us
    reshape x2, local copies, waits for them, and re-layouts, dedispersion_factors(): doubled = jnp.broadcast_to(shifts.reshape(trials, devices, 1, local), (tr...  3.87 us
    pallas_call x1, Pallas kernels, bin_powers(): pl.pallas_call(powers_kernel, in_specs=[pl.BlockSpec(memory_space=pl.ANY)...  2.78 us
    broadcast_in_dim x2, local copies, waits for them, and re-layouts, dedispersion_factors(): jnp.broadcast_to(shifts.reshape(trials, devices, 1, local), (trials, devi...  2.12 us
  transfers between devices with their start and end apart: 1, of which 1 were waited for; matrix products, arithmetic and copies ran while one was open for 8% of the time, Pallas kernels for 7%

profile of v4, /device:TPU:1, one launch (start us, length us, event | category | flops | bytes accessed | tf_op | source)
XLA Modules:
  0.0 80.8 jit_solution(99999824516813231)
XLA Ops:
  0.0 16.1 %spectra.1 = bf16[128,16,512]{2,1,0:T(8,128)(2,1)} custom-call(s32[1]{0:T(128)} %bitcast.1.refs_0_, s32[64,512]{1,0:T(8,128)} %refs_1_.1, bf16[512,512]{1,0:T(8,128)(2,1)} %constant.14.clone.refs_2_, bf16[4,4096,128]{2,1,0:T(8,128)(2,1)} %refs_3_.1), custom_call_target="tpu_custom_call" | custom-call | tf_op jit(solution)/shard_map/spectra/pallas_call | solution.py:91
  16.1 0.0 copy-start
  16.1 11.5 %all-to-all-start = ((bf16[128,16,512]{2,1,0:T(8,128)(2,1)}), bf16[128,16,512]{2,1,0:T(8,128)(2,1)S(1)}, u32[]{:S(2)}, u32[]{:S(2)}) async-start(bf16[128,16,512]{2,1,0:T(8,128)(2,1)} %spectra.1), calls=%async_computation | async-start | bytes 4194304 | tf_op jit(solution)/shard_map/all_to_all | solution.py:261
  27.6 0.0 copy-done
  27.6 0.2 copy.5
  27.8 0.9 %broadcast_in_dim.7 = s32[256,128,4]{0,2,1:T(4,128)} reshape(s32[256,512]{0,1:T(8,128)S(1)} %copy.5) | data formatting | bytes 1048576 | tf_op jit(solution)/shard_map/broadcast_in_dim | solution.py:131
  28.8 1.2 %broadcast_in_dim.8 = s32[256,128,2,4]{0,3,2,1:T(4,128)S(1)} broadcast(s32[256,128,4]{0,2,1:T(4,128)} %broadcast_in_dim.7), dimensions={0,1,3} | broadcast | bytes 1572864 | tf_op jit(solution)/shard_map/broadcast_in_dim | solution.py:131
  29.9 1.3 %reshape.15 = s32[256,1024]{0,1:T(8,128)} reshape(s32[256,128,2,4]{0,3,2,1:T(4,128)S(1)} %broadcast_in_dim.8) | data formatting | bytes 2097152 | tf_op jit(solution)/shard_map/reshape | solution.py:133
  31.3 2.5 %copy.6.refs_1_ = s32[256,1024]{1,0:T(8,128)} copy(s32[256,1024]{0,1:T(8,128)} %reshape.15) | data formatting | bytes 2097152 | tf_op jit(solution)/shard_map/reshape | solution.py:133
  33.8 5.6 %factors.1.stored = bf16[2,512,1024]{2,1,0:T(8,128)(2,1)} custom-call(s32[1]{0:T(128)} %bitcast.refs_0_, s32[256,1024]{1,0:T(8,128)} %copy.6.refs_1_), custom_call_target="tpu_custom_call" | custom-call | tf_op jit(solution)/shard_map/factors/pallas_call | solution.py:134
  39.4 18.0 %all-to-all-done.spec = bf16[128,16,512]{2,1,0:T(8,128)(2,1)S(1)} async-done(((bf16[128,16,512]{2,1,0:T(8,128)(2,1)}), bf16[128,16,512]{2,1,0:T(8,128)(2,1)S(1)}, u32[]{:S(2)}, u32[]{:S(2)}) %all-to-all-start) | async-done | bytes 2097184 | tf_op jit(solution)/shard_map/all_to_all | solution.py:261
  57.3 2.8 %powers.1 = bf16[32,4,16,128]{3,2,1,0:T(8,128)(2,1)S(1)} custom-call(bf16[2,512,1024]{2,1,0:T(8,128)(2,1)} %factors.1.stored, bf16[128,16,512]{2,1,0:T(8,128)(2,1)S(1)} %all-to-all-done.spec), custom_call_target="tpu_custom_call" | custom-call | tf_op jit(solution)/shard_map/powers/pallas_call | solution.py:187
  60.1 18.6 %all_to_all.10.moved = bf16[128,16,128]{2,1,0:T(8,128)(2,1)S(1)} all-to-all(bf16[128,16,128]{2,1,0:T(8,128)(2,1)S(1)} %bitcast.7), channel_id=1, replica_groups=mesh['chan'=32,'grp'=4] {'chan','grp'}, dimensions={0} | all-to-all | bytes 1048576 | tf_op jit(solution)/shard_map/all_to_all | solution.py:265
  78.7 2.1 %arrange.1 = f32[64,16,256]{2,1,0:T(8,128)} custom-call(bf16[128,16,128]{2,1,0:T(8,128)(2,1)S(1)} %all_to_all.10.moved), custom_call_target="tpu_custom_call" | custom-call | tf_op jit(solution)/shard_map/arrange/pallas_call | solution.py:230
Async XLA Ops:
  16.1 11.5 %copy-start = (s32[256,512]{1,0:T(8,128)S(1)}, s32[256,512]{1,0:T(8,128)}, u32[]{:S(2)}) copy-start(s32[256,512]{1,0:T(8,128)} %param.6) | copy-start | bytes 1572868
  16.1 41.2 %all-to-all-start = ((bf16[128,16,512]{2,1,0:T(8,128)(2,1)}), bf16[128,16,512]{2,1,0:T(8,128)(2,1)S(1)}, u32[]{:S(2)}, u32[]{:S(2)}) async-start(bf16[128,16,512]{2,1,0:T(8,128)(2,1)} %spectra.1), calls=%async_computation | async-start | bytes 4194304 | tf_op jit(solution)/shard_map/all_to_all | solution.py:261

commit v5 on v4

--- a/solution.py
+++ b/solution.py
@@ -11,6 +11,7 @@
 INTEG = 8
 PHASES = 4096
 BLOCKS = 8
+PIECES = 8
 VMEM_LIMIT = 56 * 1024 * 1024
 PARAMS = pltpu.CompilerParams(vmem_limit_bytes=VMEM_LIMIT)
 
@@ -31,9 +32,18 @@
     return sine, cosine
 
 
-def spectra_kernel(first, delays, table, volts, out, spread, rows, weights, series, mixed, *, total):
+def spectra_kernel(
+    first, delays, stored, volts, out, spread, rows, weights, series, mixed, staged, table, arrived,
+    written, *, total
+):
     dishes, beams = delays.shape
     channel = pl.program_id(0)
+    fetch = pltpu.make_async_copy(stored, table, arrived)
+
+    @pl.when(channel == 0)
+    def _():
+        fetch.start()
+
     sine, cosine = sin_cos(delays[...] * (first[0] + channel + total), PHASES)
     scale = jnp.float32(1.0 / math.sqrt(dishes))
     real = (cosine * scale).astype(jnp.bfloat16)
@@ -62,6 +72,11 @@
             series[tb * piece : (tb + 1) * piece, n * width : (n + 1) * width] = mean.astype(
                 jnp.bfloat16
             )
+
+    @pl.when(channel == 0)
+    def _():
+        fetch.wait()
+
     result = jnp.dot(table[...], series[...], preferred_element_type=jnp.float32)
     owners, share, _ = out.shape
     kinds = result.shape[0] // owners
@@ -76,10 +91,19 @@
 
     @pl.when(channel == pl.num_programs(0) - 1)
     def _():
-        for n in range(tiles):
-            out[:, :, n * width : (n + 1) * width] = (
-                mixed[n].reshape(owners, share, width).astype(jnp.bfloat16)
-            )
+        count = owners // PIECES
+        copies = []
+        for q in range(PIECES):
+            span = slice(q * count, (q + 1) * count)
+            for n in range(tiles):
+                piece = mixed[n, q * count * share : (q + 1) * count * share, :]
+                staged[span, :, n * width : (n + 1) * width] = piece.reshape(
+                    count, share, width
+                ).astype(jnp.bfloat16)
+            copies.append(pltpu.make_async_copy(staged.at[span], out.at[span], written.at[q]))
+            copies[-1].start()
+        for copy in copies:
+            copy.wait()
 
 
 def spectra(voltages, delays, table, first, total, devices):
@@ -94,10 +118,10 @@
         in_specs=[
             pl.BlockSpec(memory_space=pltpu.SMEM),
             pl.BlockSpec((dishes, beams), lambda i: (0, 0)),
-            pl.BlockSpec((steps, steps), lambda i: (0, 0)),
+            pl.BlockSpec(memory_space=pl.ANY),
             pl.BlockSpec((1, time, doubled), lambda i: (i, 0, 0)),
         ],
-        out_specs=pl.BlockSpec((devices, share, beams), lambda i: (0, 0, 0)),
+        out_specs=pl.BlockSpec(memory_space=pl.ANY),
         out_shape=jax.ShapeDtypeStruct((devices, share, beams), jnp.bfloat16),
         scratch_shapes=[
             pltpu.VMEM((time, doubled), jnp.float32),
@@ -105,6 +129,10 @@
             pltpu.VMEM((beams // width, doubled, 2 * width), jnp.bfloat16),
             pltpu.VMEM((steps, beams), jnp.bfloat16),
             pltpu.VMEM((beams // width, devices * share, width), jnp.float32),
+            pltpu.VMEM((devices, share, beams), jnp.bfloat16),
+            pltpu.VMEM((steps, steps), jnp.bfloat16),
+            pltpu.SemaphoreType.DMA,
+            pltpu.SemaphoreType.DMA((PIECES,)),
         ],
         compiler_params=PARAMS,
         name="spectra",

time: 81.1 us -> 81.4 us (level)
  no operation moved by 1% of the time
where the time goes in v5:
time: 81.4 us; the launch traced here: 81.1 us
  Pallas kernels  26.8 us (33%)
  blocking collectives  18.6 us (23%)
  waiting for transfers between devices  18 us (22%)
  starting transfers between devices  11.5 us (14%)
  local copies, waits for them, and re-layouts  6.19 us (8%)
    all_to_all x1, blocking collectives, body(): lax.all_to_all(powers, both, split_axis=0, concat_axis=0, tiled=True)  18.6 us
    all_to_all x1, waiting for transfers between devices, body(): spec = lax.all_to_all(sent, both, split_axis=0, concat_axis=0, tiled=True)  18 us
    pallas_call x1, Pallas kernels, spectra(): pl.pallas_call(lambda *refs: spectra_kernel(*refs, total=total), grid=(lo...  16.3 us
    all_to_all x1, starting transfers between devices, body(): spec = lax.all_to_all(sent, both, split_axis=0, concat_axis=0, tiled=True)  11.5 us
    pallas_call x1, Pallas kernels, dedispersion_factors(): pl.pallas_call(lambda *refs: factors_kernel(*refs, devices=devices, lengt...  5.57 us
    reshape x2, local copies, waits for them, and re-layouts, dedispersion_factors(): doubled = jnp.broadcast_to(shifts.reshape(trials, devices, 1, local), (tr...  3.87 us
    pallas_call x1, Pallas kernels, bin_powers(): pl.pallas_call(powers_kernel, in_specs=[pl.BlockSpec(memory_space=pl.ANY)...  2.79 us
    broadcast_in_dim x2, local copies, waits for them, and re-layouts, dedispersion_factors(): jnp.broadcast_to(shifts.reshape(trials, devices, 1, local), (trials, devi...  2.12 us
  transfers between devices with their start and end apart: 1, of which 1 were waited for; matrix products, arithmetic and copies ran while one was open for 8% of the time, Pallas kernels for 7%

profile of v5, /device:TPU:1, one launch (start us, length us, event | category | flops | bytes accessed | tf_op | source)
XLA Modules:
  0.0 81.1 jit_solution(4302947534378584590)
XLA Ops:
  0.0 16.3 %spectra.1 = bf16[128,16,512]{2,1,0:T(8,128)(2,1)} custom-call(s32[1]{0:T(128)} %bitcast.1.refs_0_, s32[64,512]{1,0:T(8,128)} %refs_1_.1, bf16[512,512]{1,0:T(8,128)(2,1)} %constant.14.clone.refs_2_, bf16[4,4096,128]{2,1,0:T(8,128)(2,1)} %refs_3_.1), custom_call_target="tpu_custom_call" | custom-call | tf_op jit(solution)/shard_map/spectra/pallas_call | solution.py:115
  16.4 0.0 copy-start
  16.4 11.5 %all-to-all-start = ((bf16[128,16,512]{2,1,0:T(8,128)(2,1)}), bf16[128,16,512]{2,1,0:T(8,128)(2,1)S(1)}, u32[]{:S(2)}, u32[]{:S(2)}) async-start(bf16[128,16,512]{2,1,0:T(8,128)(2,1)} %spectra.1), calls=%async_computation | async-start | bytes 4194304 | tf_op jit(solution)/shard_map/all_to_all | solution.py:289
  27.9 0.0 copy-done
  27.9 0.2 copy.5
  28.1 0.9 %broadcast_in_dim.7 = s32[256,128,4]{0,2,1:T(4,128)} reshape(s32[256,512]{0,1:T(8,128)S(1)} %copy.5) | data formatting | bytes 1048576 | tf_op jit(solution)/shard_map/broadcast_in_dim | solution.py:159
  29.0 1.2 %broadcast_in_dim.8 = s32[256,128,2,4]{0,3,2,1:T(4,128)S(1)} broadcast(s32[256,128,4]{0,2,1:T(4,128)} %broadcast_in_dim.7), dimensions={0,1,3} | broadcast | bytes 1572864 | tf_op jit(solution)/shard_map/broadcast_in_dim | solution.py:159
  30.2 1.3 %reshape.15 = s32[256,1024]{0,1:T(8,128)} reshape(s32[256,128,2,4]{0,3,2,1:T(4,128)S(1)} %broadcast_in_dim.8) | data formatting | bytes 2097152 | tf_op jit(solution)/shard_map/reshape | solution.py:161
  31.5 2.5 %copy.6.refs_1_ = s32[256,1024]{1,0:T(8,128)} copy(s32[256,1024]{0,1:T(8,128)} %reshape.15) | data formatting | bytes 2097152 | tf_op jit(solution)/shard_map/reshape | solution.py:161
  34.1 5.6 %factors.1.stored = bf16[2,512,1024]{2,1,0:T(8,128)(2,1)} custom-call(s32[1]{0:T(128)} %bitcast.refs_0_, s32[256,1024]{1,0:T(8,128)} %copy.6.refs_1_), custom_call_target="tpu_custom_call" | custom-call | tf_op jit(solution)/shard_map/factors/pallas_call | solution.py:162
  39.6 18.0 %all-to-all-done.spec = bf16[128,16,512]{2,1,0:T(8,128)(2,1)S(1)} async-done(((bf16[128,16,512]{2,1,0:T(8,128)(2,1)}), bf16[128,16,512]{2,1,0:T(8,128)(2,1)S(1)}, u32[]{:S(2)}, u32[]{:S(2)}) %all-to-all-start) | async-done | bytes 2097184 | tf_op jit(solution)/shard_map/all_to_all | solution.py:289
  57.6 2.8 %powers.1 = bf16[32,4,16,128]{3,2,1,0:T(8,128)(2,1)S(1)} custom-call(bf16[2,512,1024]{2,1,0:T(8,128)(2,1)} %factors.1.stored, bf16[128,16,512]{2,1,0:T(8,128)(2,1)S(1)} %all-to-all-done.spec), custom_call_target="tpu_custom_call" | custom-call | tf_op jit(solution)/shard_map/powers/pallas_call | solution.py:215
  60.4 18.6 %all_to_all.10.moved = bf16[128,16,128]{2,1,0:T(8,128)(2,1)S(1)} all-to-all(bf16[128,16,128]{2,1,0:T(8,128)(2,1)S(1)} %bitcast.7), channel_id=1, replica_groups=mesh['chan'=32,'grp'=4] {'chan','grp'}, dimensions={0} | all-to-all | bytes 1048576 | tf_op jit(solution)/shard_map/all_to_all | solution.py:293
  79.0 2.1 %arrange.1 = f32[64,16,256]{2,1,0:T(8,128)} custom-call(bf16[128,16,128]{2,1,0:T(8,128)(2,1)S(1)} %all_to_all.10.moved), custom_call_target="tpu_custom_call" | custom-call | tf_op jit(solution)/shard_map/arrange/pallas_call | solution.py:258
Async XLA Ops:
  16.4 11.5 %copy-start = (s32[256,512]{1,0:T(8,128)S(1)}, s32[256,512]{1,0:T(8,128)}, u32[]{:S(2)}) copy-start(s32[256,512]{1,0:T(8,128)} %param.6) | copy-start | bytes 1572868
  16.4 41.2 %all-to-all-start = ((bf16[128,16,512]{2,1,0:T(8,128)(2,1)}), bf16[128,16,512]{2,1,0:T(8,128)(2,1)S(1)}, u32[]{:S(2)}, u32[]{:S(2)}) async-start(bf16[128,16,512]{2,1,0:T(8,128)(2,1)} %spectra.1), calls=%async_computation | async-start | bytes 4194304 | tf_op jit(solution)/shard_map/all_to_all | solution.py:289
